TPU v7x, 512 devices: a whole 4x8x8 slice. The times are simulated.
512 devices in a mesh: req: 64 (over z_lo, x, y), tp: 8 (over z_hi, core).
Axes of the slice: x: 4, y: 8, z: 8 (z_hi: 4, z_lo: 2; z = z_hi * 2 + z_lo), core: 2. Of those that a mesh axis runs over, the one named last changes fastest.
Arguments:
- q_proj: bfloat16 [64, 128, 3072], P('req', None, 'tp'), may hold values from -24 to 24, as said below
- kv_proj: bfloat16 [64, 128, 2, 1024], P('req', None, None, 'tp'), may hold values from -6 to 6
- q_bias: bfloat16 [3072], P('tp'), may hold values from -3 to 3
- kv_bias: bfloat16 [2, 1024], P(None, 'tp'), may hold values from -3 to 3
- prefix_kv: bfloat16 [64, 1024, 2, 1024], P('req', None, None, 'tp'), may hold values from -24 to 24, as said below
- lengths: int32 [64], P('req'), may hold values from 1 to 128, 4096 in all
- group_of: int32 [64], P('req'), may hold values from 0 to 2
- owner: int32 [3], replicated, may hold values from 0 to 63
- positions: int32 [64, 128], P('req'), may hold values from 1024 to 1278, as said below
- residual: bfloat16 [64, 128, 5120], P('req', None, 'tp'), may hold values from -6 to 6
- out_weight: bfloat16 [3072, 5120], P(None, 'tp'), may hold values from -0.109375 to 0.109375
Outputs:
- hidden: bfloat16 [64, 128, 5120], P('req', None, 'tp')
Inputs may be any that keep to these rules, and one draw needn't show every extreme that they name: `q_proj`: projected queries; entries stay within the stated bounds. `prefix_kv`: cached keys are already rotated at prefix positions 0 to 1023. Each request's positions are a start of 1024 or more plus the slot index.
All inputs are finite; a program needn't handle non-finite values. No bound on the sum of `lengths` on one device may be relied on, other than what follows from the above.
Results may differ from a plain program's by a relative error of at most 0.006.
Values may be sent and summed in bfloat16 or wider, within the bound.
No kernel may reach another device: no remote copies, remote signals or barrier semaphores. Data moves between devices by JAX's collectives and lax.ppermute only.
A program may use at most 128 MiB of HBM per device.

v0:
```python
import math

import jax
import jax.numpy as jnp
from jax import lax
from jax.sharding import PartitionSpec as P

HD = 128


def spread(x, axis, root):
    mine = lax.axis_index(axis) == root
    return lax.psum(jnp.where(mine, x, jnp.zeros_like(x)), axis)


def rotate(vectors, places):
    half = HD // 2
    index = jnp.arange(half).astype(jnp.float32)
    freqs = jnp.exp(index * (-2.0 / HD) * math.log(1000000.0))
    angles = places.astype(jnp.float32)[:, None] * freqs[None, :]
    cosine = jnp.concatenate([jnp.cos(angles), jnp.cos(angles)], axis=-1)[:, None, :]
    sine = jnp.concatenate([jnp.sin(angles), jnp.sin(angles)], axis=-1)[:, None, :]
    turned = jnp.concatenate([-vectors[..., half:], vectors[..., :half]], axis=-1)
    return vectors * cosine + turned * sine


def attend_rows(queries, all_keys, all_vals, length, prefix_len):
    count = queries.shape[0]
    slots = jnp.arange(count)
    causal = slots[None, :] <= slots[:, None]
    allowed = jnp.concatenate([jnp.ones((count, prefix_len), dtype=bool), causal], axis=1)
    scores = jnp.einsum("rhd,kd->hrk", queries, all_keys, preferred_element_type=jnp.float32) * (
        1.0 / math.sqrt(HD)
    )
    scores = jnp.where(allowed[None], scores, -1e30)
    top = jnp.max(scores, axis=-1, keepdims=True)
    weights = jnp.where(allowed[None], jnp.exp(scores - top), 0.0)
    total = jnp.sum(weights, axis=-1)
    rounded = weights.astype(jnp.bfloat16)
    mixed = jnp.einsum("hrk,kd->rhd", rounded, all_vals, preferred_element_type=jnp.float32)
    mixed = mixed / jnp.transpose(total)[:, :, None]
    mixed = jnp.where((slots < length)[:, None, None], mixed, 0.0)
    return mixed.astype(jnp.bfloat16)


def body(
    q_proj,
    kv_proj,
    q_bias,
    kv_bias,
    prefix_kv,
    lengths,
    group_of,
    owner,
    positions,
    residual,
    out_weight,
):
    cap = q_proj.shape[1]
    prefix_len = prefix_kv.shape[1]
    mine = group_of[0]
    length = lengths[0]
    places = positions[0]
    queries = q_proj[0].astype(jnp.float32).reshape(cap, -1, HD) + q_bias.astype(
        jnp.float32
    ).reshape(-1, HD)
    queries = rotate(queries, places).astype(jnp.bfloat16)
    pairs = kv_proj[0].astype(jnp.float32) + kv_bias.astype(jnp.float32)
    keys = rotate(pairs[:, 0][:, None, :], places)[:, 0].astype(jnp.bfloat16)
    vals = pairs[:, 1].astype(jnp.bfloat16)
    slab = jnp.zeros_like(prefix_kv[0])
    for group in range(owner.shape[0]):
        received = spread(prefix_kv[0], "req", owner[group])
        slab = jnp.where(mine == group, received, slab)
    all_keys = jnp.concatenate([slab[:, 0], keys], axis=0)
    all_vals = jnp.concatenate([slab[:, 1], vals], axis=0)
    attended = attend_rows(queries, all_keys, all_vals, length, prefix_len)
    attended = attended.reshape(cap, -1)
    whole_heads = lax.all_gather(attended, "tp", axis=1, tiled=True)
    projected = jnp.dot(whole_heads, out_weight, preferred_element_type=jnp.float32)
    hidden = (residual[0].astype(jnp.float32) + projected).astype(jnp.bfloat16)
    return hidden[None]


def solution(mesh):
    in_specs = (
        P("req", None, "tp"),
        P("req", None, None, "tp"),
        P("tp"),
        P(None, "tp"),
        P("req", None, None, "tp"),
        P("req"),
        P("req"),
        P(),
        P("req", None),
        P("req", None, "tp"),
        P(None, "tp"),
    )
    out_specs = P("req", None, "tp")
    return jax.shard_map(body, mesh=mesh, in_specs=in_specs, out_specs=out_specs, check_vma=False)
```

profile of v0, /device:TPU:1, one launch (start us, length us, event | category | flops | bytes accessed | tf_op | source)
XLA Modules:
  0.0 664.5 jit_solution(9709575429134257465)
XLA Ops:
  6.5 0.0 all-reduce.4.cloned.1.call-start
  6.5 1.4 fusion.31
  9.9 0.0 copy-start.4
  9.9 0.0 copy-start.1
  9.9 2.3 select_bitcast_fusion
  12.2 0.0 copy-start.5
  12.2 0.0 copy-start.2
  12.2 0.0 copy-start.3
  12.2 0.0 all-reduce.4.cloned.1.call-update
  12.9 0.0 copy-done.4
  12.9 0.3 fusion.22
  13.3 0.1 pad_maximum_fusion
  13.4 0.1 copy.24
  13.5 0.1 copy.25
  13.6 0.0 copy-done.1
  13.6 0.1 copy.23
  13.7 0.0 copy-done.5
  14.4 0.0 copy-done.2
  14.5 0.0 copy-done.3
  14.5 0.1 slice_negate_fusion.1
  14.6 0.1 fusion.21
  14.7 0.1 convert_add_fusion
  14.9 0.1 fusion.17
  15.0 570.6 %all-reduce.4.cloned.1.call-done = (bf16[1024,2,128]{2,0,1:T(8,128)(2,1)}, bf16[1024,2,128]{2,0,1:T(8,128)(2,1)}, bf16[1024,2,128]{2,0,1:T(8,128)(2,1)}) async-done(((bf16[1024,2,128]{2,0,1:T(8,128)(2,1)}, bf16[1024,2,128]{2,0,1:T(8,128)(2,1)}, bf16[1024,2,128]{2,0,1:T(8,128)(2,1)}), (bf16[1024,2,128]{2,0,1:T(8,128)(2,1)}, bf16[1024,2,128]{2,0,1:T(8,128)(2,1)}, ...) | async-done | bytes 1572880 | tf_op jit(solution)/shard_map/psum | solution.py:13
  585.6 1.1 select_select_fusion
  586.7 0.9 fusion.32
  587.7 0.4 fusion.3
  588.1 0.0 copy-start
  588.1 0.6 fusion.10
  588.7 65.4 %all_gather.3 = bf16[128,3072]{0,1:T(8,128)(2,1)S(1)} all-gather(bf16[128,384]{0,1:T(8,128)(2,1)S(1)} %bitcast.78), channel_id=1, replica_groups=mesh['req'=64,'tp'=8] {'tp'}, dimensions={1}, use_global_device_ids=true | all-gather | bytes 884736 | tf_op jit(solution)/shard_map/all_gather | solution.py:79
  654.1 0.0 copy-done
  654.1 3.6 fusion.9
  (11 shorter events, 0.2 us)
Async XLA Ops:
  6.5 579.0 %all-reduce.4.cloned.1.call-start = ((), (), s32[]{:S(2)}) async-start(), calls=%async_computation | async-start | bytes 3145728 | tf_op jit(solution)/shard_map/psum | solution.py:13
  9.9 3.1 copy-start.4
  9.9 3.7 copy-start.1
  12.2 1.5 copy-start.5
  12.2 2.2 copy-start.2
  12.2 2.3 copy-start.3
  588.1 66.0 %copy-start = (bf16[1,128,640]{2,1,0:T(8,128)(2,1)S(1)}, bf16[1,128,640]{2,1,0:T(8,128)(2,1)}, u32[]{:S(2)}) copy-start(bf16[1,128,640]{2,1,0:T(8,128)(2,1)} %param.20) | copy-start | bytes 491524
Sparse Core Ops, SparseCore 0:
  12.4 573.1 all-reduce.3
where the time goes:
time: 665 us
  waiting for transfers between devices  571 us (86%)
  blocking collectives  65.4 us (10%)
  between operations  16.8 us (3%)
    psum x1, waiting for transfers between devices, spread(): return lax.psum(jnp.where(mine, x, jnp.zeros_like(x)), axis)  571 us
    all_gather x1, blocking collectives, body(): whole_heads = lax.all_gather(attended, 'tp', axis=1, tiled=True)  65.4 us
  transfers between devices with their start and end apart: 1, of which 1 were waited for; matrix products, arithmetic and copies ran while one was open for 0% of the time, Pallas kernels for 0%

commit v1 on v0

--- a/solution.py
+++ b/solution.py
@@ -6,11 +6,6 @@
 from jax.sharding import PartitionSpec as P
 
 HD = 128
-
-
-def spread(x, axis, root):
-    mine = lax.axis_index(axis) == root
-    return lax.psum(jnp.where(mine, x, jnp.zeros_like(x)), axis)
 
 
 def rotate(vectors, places):
@@ -22,6 +17,23 @@
     sine = jnp.concatenate([jnp.sin(angles), jnp.sin(angles)], axis=-1)[:, None, :]
     turned = jnp.concatenate([-vectors[..., half:], vectors[..., :half]], axis=-1)
     return vectors * cosine + turned * sine
+
+
+def fetch_prefix(slab, group, owner):
+    columns = lax.axis_size("req")
+    piece = slab.shape[0] // columns
+    pieces = slab.reshape(columns, piece, 2, HD)
+    tag = jnp.broadcast_to(group.astype(slab.dtype), (columns, 1, 2, HD))
+    spread = lax.all_to_all(jnp.concatenate([pieces, tag], axis=1), "req", 0, 0, tiled=True)
+    groups = spread[:, piece, 0, 0].astype(jnp.int32)
+    owned = [
+        jnp.swapaxes(lax.dynamic_index_in_dim(spread, owner[g], 0, keepdims=False)[:piece], 0, 1)
+        for g in range(owner.shape[0])
+    ]
+    outgoing = jnp.broadcast_to(owned[0], (columns, 2, piece, HD))
+    for g in range(1, owner.shape[0]):
+        outgoing = jnp.where((groups == g)[:, None, None, None], owned[g][None], outgoing)
+    return lax.all_to_all(outgoing, "req", 0, 0, tiled=True)
 
 
 def attend_rows(queries, all_keys, all_vals, length, prefix_len):
@@ -58,9 +70,9 @@
 ):
     cap = q_proj.shape[1]
     prefix_len = prefix_kv.shape[1]
-    mine = group_of[0]
     length = lengths[0]
     places = positions[0]
+    slab = fetch_prefix(prefix_kv[0], group_of[0], owner)
     queries = q_proj[0].astype(jnp.float32).reshape(cap, -1, HD) + q_bias.astype(
         jnp.float32
     ).reshape(-1, HD)
@@ -68,12 +80,8 @@
     pairs = kv_proj[0].astype(jnp.float32) + kv_bias.astype(jnp.float32)
     keys = rotate(pairs[:, 0][:, None, :], places)[:, 0].astype(jnp.bfloat16)
     vals = pairs[:, 1].astype(jnp.bfloat16)
-    slab = jnp.zeros_like(prefix_kv[0])
-    for group in range(owner.shape[0]):
-        received = spread(prefix_kv[0], "req", owner[group])
-        slab = jnp.where(mine == group, received, slab)
-    all_keys = jnp.concatenate([slab[:, 0], keys], axis=0)
-    all_vals = jnp.concatenate([slab[:, 1], vals], axis=0)
+    all_keys = jnp.concatenate([slab[:, 0].reshape(prefix_len, HD), keys], axis=0)
+    all_vals = jnp.concatenate([slab[:, 1].reshape(prefix_len, HD), vals], axis=0)
     attended = attend_rows(queries, all_keys, all_vals, length, prefix_len)
     attended = attended.reshape(cap, -1)
     whole_heads = lax.all_gather(attended, "tp", axis=1, tiled=True)

time: 665 us -> 90 us (0.14)
  waiting for transfers between devices: 571 us -> 24.4 us
  blocking collectives: 65.4 us -> 24.6 us
  starting transfers between devices: 0.01 us -> 19.2 us
  between operations: 16.8 us -> 7.34 us
    psum x1 -> x0, waiting for transfers between devices: 571 us -> none  [spread(): return lax.psum(jnp.where(mine, x, jnp.zeros_like(x)), axis)]
    all_gather x1, blocking collectives: 65.4 us -> 24.6 us  [body(): whole_heads = lax.all_gather(attended, 'tp', axis=1, tiled=True)]
    all_to_all x0 -> x2, waiting for transfers between devices: none -> 24.4 us  [the longest x1 15.3 us: fetch_prefix(): return lax.all_to_all(outgoing, 'req', 0, 0, tiled=True)]
    all_to_all x0 -> x2, starting transfers between devices: none -> 19.2 us  [the longest x1 12.9 us: fetch_prefix(): lax.all_to_all(jnp.concatenate([pieces, tag], axis=1), 'req', 0, 0, tiled...]
  transfers between devices with their start and end apart: 1 -> 2, of which waited for: 1 -> 2; matrix products, arithmetic and copies ran while one was open for 0% -> 2% of each run, Pallas kernels for 0% -> 0%
where the time goes in v1:
time: 90 us; the launch traced here: 89.6 us
  blocking collectives  24.6 us (27%)
  waiting for transfers between devices  24.4 us (27%)
  starting transfers between devices  19.2 us (21%)
  between operations  7.34 us (8%)
  matrix products  5.58 us (6%)
  other arithmetic  4.3 us (5%)
  local copies, waits for them, and re-layouts  4.2 us (5%)
    all_gather x1, blocking collectives, body(): whole_heads = lax.all_gather(attended, 'tp', axis=1, tiled=True)  24.6 us
    all_to_all x1, waiting for transfers between devices, fetch_prefix(): return lax.all_to_all(outgoing, 'req', 0, 0, tiled=True)  15.3 us
    all_to_all x1, starting transfers between devices, fetch_prefix(): lax.all_to_all(jnp.concatenate([pieces, tag], axis=1), 'req', 0, 0, tiled...  12.9 us
    all_to_all x1, waiting for transfers between devices, fetch_prefix(): lax.all_to_all(jnp.concatenate([pieces, tag], axis=1), 'req', 0, 0, tiled...  9.09 us
    all_to_all x1, starting transfers between devices, fetch_prefix(): return lax.all_to_all(outgoing, 'req', 0, 0, tiled=True)  6.25 us
    dot_general x1, matrix products, body(): jnp.dot(whole_heads, out_weight, preferred_element_type=jnp.float32)  3.62 us
    eq x1, other arithmetic, fetch_prefix(): groups == g  2.39 us
    unnamed x18, local copies, waits for them, and re-layouts  1.82 us
  transfers between devices with their start and end apart: 2, of which 2 were waited for; matrix products, arithmetic and copies ran while one was open for 2% of the time, Pallas kernels for 0%

profile of v1, /device:TPU:1, one launch (start us, length us, event | category | flops | bytes accessed | tf_op | source)
XLA Modules:
  0.0 89.6 jit_solution(15967355962080478842)
XLA Ops:
  0.0 1.1 %copy.38 = bf16[1,1024,2,128]{3,1,2,0:T(8,128)(2,1)S(1)} copy(bf16[1,1024,2,128]{3,2,1,0:T(2,128)(2,1)} %param.15) | data formatting | bytes 1048576 | tf_op args[4]
  1.1 0.0 copy-start.3
  1.1 0.0 copy-start.5
  1.1 0.0 copy-start.2
  1.1 0.0 copy-start.1
  1.2 0.0 copy-start.6
  1.2 0.5 copy.61
  2.4 0.0 copy-start.4
  2.4 1.2 %concatenate.45.clone = bf16[64,17,2,128]{3,2,1,0:T(2,128)(2,1)} pad(bf16[64,16,2,128]{3,2,1,0:T(2,128)(2,1)S(1)} %copy.61, bf16[]{:T(256)} %bitcast.3), padding=0_0x0_1x0_0x0_0 | pad | bytes 1081346 | tf_op jit(solution)/shard_map/concatenate | solution.py:27
  3.6 12.9 %all-to-all-start = ((bf16[64,17,2,128]{3,2,1,0:T(2,128)(2,1)}), bf16[64,17,2,128]{3,2,1,0:T(2,128)(2,1)S(1)}, u32[]{:S(2)}, u32[]{:S(2)}) async-start(bf16[64,17,2,128]{3,2,1,0:T(2,128)(2,1)} %concatenate.45.clone), calls=%async_computation | async-start | bytes 1114112 | tf_op jit(solution)/shard_map/all_to_all | solution.py:27
  16.5 0.0 copy-done.3
  16.5 0.6 fusion.32
  21.0 0.0 copy-done.5
  21.0 0.0 copy-done.2
  21.1 0.1 copy.46
  21.2 0.0 copy-done.1
  21.2 0.1 copy.47
  21.3 0.0 copy-done.6
  21.3 0.3 fusion.22
  21.6 0.1 pad_maximum_fusion
  21.7 0.1 copy.49
  21.8 0.1 copy.48
  24.6 0.0 copy-done.4
  24.6 0.1 slice_negate_fusion.1
  24.7 9.1 %all-to-all-done = bf16[64,17,2,128]{3,2,1,0:T(2,128)(2,1)S(1)} async-done(((bf16[64,17,2,128]{3,2,1,0:T(2,128)(2,1)}), bf16[64,17,2,128]{3,2,1,0:T(2,128)(2,1)S(1)}, u32[]{:S(2)}, u32[]{:S(2)}) %all-to-all-start) | async-done | bytes 557088 | tf_op jit(solution)/shard_map/all_to_all | solution.py:27
  33.8 2.4 %compare_reduce_fusion.1 = (pred[64]{0:T(512)(128)(4,1)S(1)}, pred[64]{0:T(512)(128)(4,1)S(1)}) fusion(bf16[64,17,2,128]{3,2,1,0:T(2,128)(2,1)S(1)} %all-to-all-done), kind=kLoop, calls=%fused_computation.28 | loop fusion | flops 192 | bytes 256 | tf_op jit(solution)/shard_map/eq | solution.py:35
  36.2 1.0 %select_select_fusion = bf16[64,2,16,128]{3,2,1,0:T(8,128)(2,1)} fusion(pred[64]{0:T(512)(128)(4,1)S(1)} %get-tuple-element.6, pred[64]{0:T(512)(128)(4,1)S(1)} %get-tuple-element.5, bf16[2,16,128]{2,1,0:T(8,128)(2,1)S(1)} %get-tuple-element.22, bf16[2,16,128]{2,1,0:T(8,128)(2,1)S(1)} %get-tuple-element.23, bf16[2,16,128]{2,1,0:T(8,128)(2,1)S(1)} %bitcast.89), kind=kLoop, calls=%fused_computation.15 | loop fusion | flops 524288 | bytes 548992 | tf_op jit(solution)/shard_map/jit(_where)/select_n | solution.py:35
  37.2 6.3 %all-to-all-start.1 = ((bf16[64,2,16,128]{3,2,1,0:T(8,128)(2,1)}), bf16[64,2,16,128]{3,2,1,0:T(8,128)(2,1)S(1)}, u32[]{:S(2)}, u32[]{:S(2)}) async-start(bf16[64,2,16,128]{3,2,1,0:T(8,128)(2,1)} %select_select_fusion), calls=%async_computation.1 | async-start | bytes 1048576 | tf_op jit(solution)/shard_map/all_to_all | solution.py:36
  43.5 0.1 fusion.21
  43.6 0.1 convert_add_fusion
  43.8 0.1 fusion.17
  43.9 15.3 %all-to-all-done.1 = bf16[64,2,16,128]{3,2,1,0:T(8,128)(2,1)S(1)} async-done(((bf16[64,2,16,128]{3,2,1,0:T(8,128)(2,1)}), bf16[64,2,16,128]{3,2,1,0:T(8,128)(2,1)S(1)}, u32[]{:S(2)}, u32[]{:S(2)}) %all-to-all-start.1) | async-done | bytes 524320 | tf_op jit(solution)/shard_map/all_to_all | solution.py:36
  59.2 0.4 fusion.3
  59.7 0.9 %fusion.33 = f32[3,128]{1,0:T(4,128)S(1)} fusion(bf16[128,3,128]{0,2,1:T(8,128)(2,1)S(1)} %fusion.17, pred[128,1152]{0,1:T(8,128)(4,1)S(1)} %concatenate.47, bf16[128,128]{1,0:T(8,128)(2,1)S(1)} %fusion.21, bf16[1024,128]{1,0:T(8,128)(2,1)S(1)} %bitcast.84), kind=kOutput, calls=%fused_computation.64 | convolution fusion | flops 116049024 | bytes 542208 | tf_op jit(solution)/shard_map/sub | solution.py:49
  60.6 0.1 copy.45
  60.7 0.0 copy-start
  60.7 0.6 fusion.10
  61.4 24.6 %all_gather.3 = bf16[128,3072]{0,1:T(8,128)(2,1)S(1)} all-gather(bf16[128,384]{0,1:T(8,128)(2,1)S(1)} %bitcast.88), channel_id=1, replica_groups=mesh['req'=64,'tp'=8] {'tp'}, dimensions={1}, use_global_device_ids=true | all-gather | bytes 884736 | tf_op jit(solution)/shard_map/all_gather | solution.py:87
  85.9 0.0 copy-done
  85.9 3.6 %fusion.9 = bf16[1,128,640]{2,1,0:T(8,128)(2,1)} fusion(bf16[128,3072]{0,1:T(8,128)(2,1)S(1)} %all_gather.3, bf16[3072,640]{1,0:T(8,128)(2,1)} %param.21, bf16[1,128,640]{2,1,0:T(8,128)(2,1)S(1)} %copy-done), kind=kOutput, calls=%fused_computation.12 | convolution fusion | flops 503562240 | bytes 5046272 | tf_op jit(solution)/shard_map/dot_general | solution.py:88
  (14 shorter events, 0.2 us)
Async XLA Ops:
  1.1 15.4 %copy-start.3 = (s32[3]{0:T(128)S(1)}, s32[3]{0:T(128)}, u32[]{:S(2)}) copy-start(s32[3]{0:T(128)} %param.18) | copy-start | bytes 40
  1.1 19.9 %copy-start.5 = (bf16[2,128]{1,0:T(2,128)(2,1)S(1)}, bf16[2,128]{1,0:T(2,128)(2,1)}, u32[]{:S(2)}) copy-start(bf16[2,128]{1,0:T(2,128)(2,1)} %param.14) | copy-start | bytes 1540
  1.1 19.9 %copy-start.2 = (bf16[1,128,2,128]{3,2,1,0:T(2,128)(2,1)S(1)}, bf16[1,128,2,128]{3,2,1,0:T(2,128)(2,1)}, u32[]{:S(2)}) copy-start(bf16[1,128,2,128]{3,2,1,0:T(2,128)(2,1)} %param.12) | copy-start | bytes 196612
  1.1 20.0 %copy-start.1 = (bf16[1,128,384]{2,1,0:T(8,128)(2,1)S(1)}, bf16[1,128,384]{2,1,0:T(8,128)(2,1)}, u32[]{:S(2)}) copy-start(bf16[1,128,384]{2,1,0:T(8,128)(2,1)} %param.11) | copy-start | bytes 294916
  1.2 20.1 %copy-start.6 = (s32[1,128]{1,0:T(1,128)S(1)}, s32[1,128]{1,0:T(1,128)}, u32[]{:S(2)}) copy-start(s32[1,128]{1,0:T(1,128)} %param.19) | copy-start | bytes 1540
  2.4 22.2 %copy-start.4 = (bf16[384]{0:T(512)(128)(2,1)S(1)}, bf16[384]{0:T(512)(128)(2,1)}, u32[]{:S(2)}) copy-start(bf16[384]{0:T(512)(128)(2,1)} %param.13) | copy-start | bytes 2308
  3.6 30.2 %all-to-all-start = ((bf16[64,17,2,128]{3,2,1,0:T(2,128)(2,1)}), bf16[64,17,2,128]{3,2,1,0:T(2,128)(2,1)S(1)}, u32[]{:S(2)}, u32[]{:S(2)}) async-start(bf16[64,17,2,128]{3,2,1,0:T(2,128)(2,1)} %concatenate.45.clone), calls=%async_computation | async-start | bytes 1114112 | tf_op jit(solution)/shard_map/all_to_all | solution.py:27
  37.2 22.0 %all-to-all-start.1 = ((bf16[64,2,16,128]{3,2,1,0:T(8,128)(2,1)}), bf16[64,2,16,128]{3,2,1,0:T(8,128)(2,1)S(1)}, u32[]{:S(2)}, u32[]{:S(2)}) async-start(bf16[64,2,16,128]{3,2,1,0:T(8,128)(2,1)} %select_select_fusion), calls=%async_computation.1 | async-start | bytes 1048576 | tf_op jit(solution)/shard_map/all_to_all | solution.py:36
  60.7 25.2 %copy-start = (bf16[1,128,640]{2,1,0:T(8,128)(2,1)S(1)}, bf16[1,128,640]{2,1,0:T(8,128)(2,1)}, u32[]{:S(2)}) copy-start(bf16[1,128,640]{2,1,0:T(8,128)(2,1)} %param.20) | copy-start | bytes 491524

commit v2 on v1

v2 whole, which is shorter than its diff:
```python
import functools
import math

import jax
import jax.numpy as jnp
from jax import lax
from jax.experimental import pallas as pl
from jax.experimental.pallas import tpu as pltpu
from jax.sharding import PartitionSpec as P

HD = 128
SCALE = 1.0 / math.sqrt(HD)


def rotate(vectors, places):
    half = HD // 2
    index = jnp.arange(half).astype(jnp.float32)
    freqs = jnp.exp(index * (-2.0 / HD) * math.log(1000000.0))
    angles = places.astype(jnp.float32)[:, None] * freqs[None, :]
    cosine = jnp.concatenate([jnp.cos(angles), jnp.cos(angles)], axis=-1)[:, None, :]
    sine = jnp.concatenate([jnp.sin(angles), jnp.sin(angles)], axis=-1)[:, None, :]
    turned = jnp.concatenate([-vectors[..., half:], vectors[..., :half]], axis=-1)
    return vectors * cosine + turned * sine


def tag_kernel(group_ref, slab_ref, out_ref, tag_ref, sems):
    piece = slab_ref.shape[1]
    data = pltpu.make_async_copy(slab_ref, out_ref.at[:, pl.ds(0, piece)], sems.at[0])
    data.start()
    tag_ref[...] = jnp.full(tag_ref.shape, group_ref[0].astype(jnp.float32), jnp.float32).astype(tag_ref.dtype)
    tags = pltpu.make_async_copy(tag_ref, out_ref.at[:, pl.ds(piece, 1)], sems.at[1])
    tags.start()
    data.wait()
    tags.wait()


def tagged(pieces, group):
    columns, piece = pieces.shape[:2]
    return pl.pallas_call(
        tag_kernel,
        out_shape=jax.ShapeDtypeStruct((columns, piece + 1, 2, HD), pieces.dtype),
        in_specs=[pl.BlockSpec(memory_space=pltpu.SMEM), pl.BlockSpec(memory_space=pltpu.HBM)],
        out_specs=pl.BlockSpec(memory_space=pl.ANY),
        scratch_shapes=[pltpu.VMEM((columns, 1, 2, HD), pieces.dtype), pltpu.SemaphoreType.DMA((2,))],
        compiler_params=pltpu.CompilerParams(vmem_limit_bytes=1 << 20),
        name="tag_pieces",
    )(group, pltpu.with_memory_space_constraint(pieces, pltpu.HBM))


def fetch_prefix(slab, group, owner):
    columns = lax.axis_size("req")
    piece = slab.shape[0] // columns
    pieces = slab.reshape(columns, piece, 2, HD)
    spread = lax.all_to_all(tagged(pieces, group), "req", 0, 0, tiled=True)
    groups = spread[:, piece, :, :][:, :, None, :]
    owned = [
        jnp.swapaxes(lax.dynamic_index_in_dim(spread, owner[g], 0, keepdims=False)[:piece], 0, 1)
        for g in range(owner.shape[0])
    ]
    outgoing = jnp.broadcast_to(owned[0], (columns, 2, piece, HD))
    for g in range(1, owner.shape[0]):
        outgoing = jnp.where(groups == g, owned[g][None], outgoing)
    return lax.all_to_all(outgoing, "req", 0, 0, tiled=True)


def attend_kernel(length_ref, q_ref, slab_ref, keys_ref, vals_ref, out_ref):
    heads, count, _ = q_ref.shape
    prefix_len = slab_ref.shape[0] * slab_ref.shape[2]
    over_d = (((1,), (1,)), ((), ()))
    over_k = (((1,), (0,)), ((), ()))
    prefix_keys = slab_ref[:, 0].reshape(prefix_len, HD)
    prefix_vals = slab_ref[:, 1].reshape(prefix_len, HD)
    row = lax.broadcasted_iota(jnp.int32, (count, count), 0)
    causal = lax.broadcasted_iota(jnp.int32, (count, count), 1) <= row
    live = lax.broadcasted_iota(jnp.int32, (count, HD), 0) < length_ref[0]
    for h in range(heads):
        q = q_ref[h]
        far = lax.dot_general(q, prefix_keys, over_d, preferred_element_type=jnp.float32) * SCALE
        near = lax.dot_general(q, keys_ref[...], over_d, preferred_element_type=jnp.float32) * SCALE
        near = jnp.where(causal, near, -1e30)
        top = jnp.maximum(jnp.max(far, axis=-1, keepdims=True), jnp.max(near, axis=-1, keepdims=True))
        far = jnp.exp(far - top)
        near = jnp.where(causal, jnp.exp(near - top), 0.0)
        total = jnp.sum(far, axis=-1, keepdims=True) + jnp.sum(near, axis=-1, keepdims=True)
        mixed = lax.dot_general(far.astype(jnp.bfloat16), prefix_vals, over_k, preferred_element_type=jnp.float32)
        mixed += lax.dot_general(near.astype(jnp.bfloat16), vals_ref[...], over_k, preferred_element_type=jnp.float32)
        mixed = jnp.where(live, mixed / total, 0.0)
        out_ref[:, h * HD : (h + 1) * HD] = mixed.astype(out_ref.dtype)


def attend(length, queries, slab, keys, vals):
    heads, count, _ = queries.shape
    return pl.pallas_call(
        attend_kernel,
        out_shape=jax.ShapeDtypeStruct((count, heads * HD), jnp.bfloat16),
        in_specs=[pl.BlockSpec(memory_space=pltpu.SMEM)] + [pl.BlockSpec(memory_space=pltpu.VMEM)] * 4,
        out_specs=pl.BlockSpec(memory_space=pltpu.VMEM),
        compiler_params=pltpu.CompilerParams(vmem_limit_bytes=12 << 20),
        name="attend",
    )(length, queries, slab, keys, vals)


def project_kernel(parts_ref, weight_ref, resid_ref, out_ref, held_ref, sems):
    parts, _, width = parts_ref.shape
    copies = [
        pltpu.make_async_copy(weight_ref.at[pl.ds(p * width, width)], held_ref.at[p], sems.at[p])
        for p in range(parts)
    ]
    for copy in copies:
        copy.start()
    total = resid_ref[...].astype(jnp.float32)
    for p in range(parts):
        copies[p].wait()
        total += jnp.dot(parts_ref[p], held_ref[p], preferred_element_type=jnp.float32)
    out_ref[...] = total.astype(out_ref.dtype)


def project(parts, weight, resid):
    count, _, width = parts.shape
    return pl.pallas_call(
        project_kernel,
        out_shape=jax.ShapeDtypeStruct(resid.shape, resid.dtype),
        in_specs=[
            pl.BlockSpec(memory_space=pltpu.VMEM),
            pl.BlockSpec(memory_space=pltpu.HBM),
            pl.BlockSpec(memory_space=pltpu.VMEM),
        ],
        out_specs=pl.BlockSpec(memory_space=pltpu.VMEM),
        scratch_shapes=[
            pltpu.VMEM((count, width, weight.shape[1]), weight.dtype),
            pltpu.SemaphoreType.DMA((count,)),
        ],
        compiler_params=pltpu.CompilerParams(vmem_limit_bytes=12 << 20),
        name="project",
    )(parts, pltpu.with_memory_space_constraint(weight, pltpu.HBM), resid)


def body(
    q_proj,
    kv_proj,
    q_bias,
    kv_bias,
    prefix_kv,
    lengths,
    group_of,
    owner,
    positions,
    residual,
    out_weight,
):
    cap = q_proj.shape[1]
    places = positions[0]
    slab = fetch_prefix(prefix_kv[0], group_of, owner)
    queries = q_proj[0].astype(jnp.float32).reshape(cap, -1, HD) + q_bias.astype(
        jnp.float32
    ).reshape(-1, HD)
    queries = jnp.swapaxes(rotate(queries, places).astype(jnp.bfloat16), 0, 1)
    pairs = kv_proj[0].astype(jnp.float32) + kv_bias.astype(jnp.float32)
    keys = rotate(pairs[:, 0][:, None, :], places)[:, 0].astype(jnp.bfloat16)
    vals = pairs[:, 1].astype(jnp.bfloat16)
    attended = attend(lengths, queries, slab, keys, vals)
    parts = lax.all_gather(attended, "tp", axis=0)
    return project(parts, out_weight, residual[0])[None]


def solution(mesh):
    in_specs = (
        P("req", None, "tp"),
        P("req", None, None, "tp"),
        P("tp"),
        P(None, "tp"),
        P("req", None, None, "tp"),
        P("req"),
        P("req"),
        P(),
        P("req", None),
        P("req", None, "tp"),
        P(None, "tp"),
    )
    out_specs = P("req", None, "tp")
    return jax.shard_map(body, mesh=mesh, in_specs=in_specs, out_specs=out_specs, check_vma=False)
```

time: 90 us -> 101 us (1.12)
  Pallas kernels: 0 us -> 22.2 us
  matrix products: 5.58 us -> 0 us
  waiting for transfers between devices: 24.4 us -> 20.4 us
  local copies, waits for them, and re-layouts: 4.2 us -> 2.51 us
    pallas_call x0 -> x3, Pallas kernels: none -> 22.2 us  [the longest x1 17 us: tagged(): pl.pallas_call(tag_kernel, out_shape=jax.ShapeDtypeStruct((columns, piece...]
    dot_general x3 -> x0, matrix products: 4.66 us -> none  [the longest x1 3.62 us: body(): jnp.dot(whole_heads, out_weight, preferred_element_type=jnp.float32)]
    all_to_all x1, waiting for transfers between devices: 9.09 us -> 5.2 us  [fetch_prefix(): spread = lax.all_to_all(tagged(pieces, group), 'req', 0, 0, tiled=True)]
    eq x1, other arithmetic: 2.39 us -> 0.09 us  [fetch_prefix(): outgoing = jnp.where(groups == g, owned[g][None], outgoing)]
    concatenate x4 -> x0, local copies, waits for them, and re-layouts: 1.44 us -> none  [the longest x1 1.21 us: fetch_prefix(): jnp.concatenate([pieces, tag], axis=1)]
  transfers between devices with their start and end apart: 2 -> 2, of which waited for: 2 -> 2; matrix products, arithmetic and copies ran while one was open for 2% -> 6% of each run, Pallas kernels for 0% -> 0%
where the time goes in v2:
time: 101 us
  blocking collectives  24.6 us (24%)
  Pallas kernels  22.2 us (22%)
  waiting for transfers between devices  20.4 us (20%)
  starting transfers between devices  19.2 us (19%)
  between operations  7.07 us (7%)
  other arithmetic  4.8 us (5%)
  local copies, waits for them, and re-layouts  2.51 us (2%)
    all_gather x1, blocking collectives, body(): parts = lax.all_gather(attended, 'tp', axis=0)  24.6 us
    pallas_call x1, Pallas kernels, tagged(): pl.pallas_call(tag_kernel, out_shape=jax.ShapeDtypeStruct((columns, piece...  17 us
    all_to_all x1, waiting for transfers between devices, fetch_prefix(): return lax.all_to_all(outgoing, 'req', 0, 0, tiled=True)  15.2 us
    all_to_all x1, starting transfers between devices, fetch_prefix(): spread = lax.all_to_all(tagged(pieces, group), 'req', 0, 0, tiled=True)  12.9 us
    all_to_all x1, starting transfers between devices, fetch_prefix(): return lax.all_to_all(outgoing, 'req', 0, 0, tiled=True)  6.25 us
    all_to_all x1, waiting for transfers between devices, fetch_prefix(): spread = lax.all_to_all(tagged(pieces, group), 'req', 0, 0, tiled=True)  5.2 us
    pallas_call x1, Pallas kernels, project(): pl.pallas_call(project_kernel, out_shape=jax.ShapeDtypeStruct(resid.shape...  3.81 us
  transfers between devices with their start and end apart: 2, of which 2 were waited for; matrix products, arithmetic and copies ran while one was open for 6% of the time, Pallas kernels for 0%

profile of v2, /device:TPU:1, one launch (start us, length us, event | category | flops | bytes accessed | tf_op | source)
XLA Modules:
  0.0 100.7 jit_solution(12132533480808973332)
XLA Ops:
  0.7 17.0 %tag_pieces.1 = bf16[64,17,2,128]{3,2,1,0:T(2,128)(2,1)} custom-call(s32[1]{0:T(128)S(6)} %copy.24.group_ref, bf16[64,16,2,128]{3,2,1,0:T(2,128)(2,1)} %bitcast.47), custom_call_target="tpu_custom_call" | custom-call | tf_op jit(solution)/shard_map/tag_pieces/pallas_call | solution.py:39
  17.7 12.9 %all-to-all-start = ((bf16[64,17,2,128]{3,2,1,0:T(2,128)(2,1)}), bf16[64,17,2,128]{3,2,1,0:T(2,128)(2,1)S(1)}, u32[]{:S(2)}, u32[]{:S(2)}) async-start(bf16[64,17,2,128]{3,2,1,0:T(2,128)(2,1)} %tag_pieces.1), calls=%async_computation | async-start | bytes 1114112 | tf_op jit(solution)/shard_map/all_to_all | solution.py:54
  30.6 0.0 copy-start
  30.6 1.4 %fusion.8 = (s32[1]{0:T(128)}, s32[1]{0:T(128)}, s32[1]{0:T(128)}) fusion(s32[3]{0:T(128)} %param.18), kind=kLoop, calls=%fused_computation.29 | loop fusion | bytes 24 | tf_op jit(solution)/shard_map/slice | solution.py:57
  36.4 0.7 convert_element_type.55
  37.0 0.7 bitcast_convert_fusion
  37.7 1.0 copy.16
  38.7 0.1 copy.17
  40.7 0.7 convert_bitcast_fusion
  41.4 0.3 fusion.7
  41.7 0.9 convert_add_fusion
  42.6 0.1 slice_negate_fusion.1
  42.7 5.2 %all-to-all-done = bf16[64,17,2,128]{3,2,1,0:T(2,128)(2,1)S(1)} async-done(((bf16[64,17,2,128]{3,2,1,0:T(2,128)(2,1)}), bf16[64,17,2,128]{3,2,1,0:T(2,128)(2,1)S(1)}, u32[]{:S(2)}, u32[]{:S(2)}) %all-to-all-start) | async-done | bytes 557088 | tf_op jit(solution)/shard_map/all_to_all | solution.py:54
  47.9 0.1 compare_bitcast_fusion.1
  48.0 1.0 select_select_fusion
  49.0 6.3 %all-to-all-start.1 = ((bf16[64,2,16,128]{3,2,1,0:T(8,128)(2,1)}), bf16[64,2,16,128]{3,2,1,0:T(8,128)(2,1)S(1)}, u32[]{:S(2)}, u32[]{:S(2)}) async-start(bf16[64,2,16,128]{3,2,1,0:T(8,128)(2,1)} %select_select_fusion), calls=%async_computation.1 | async-start | bytes 1048576 | tf_op jit(solution)/shard_map/all_to_all | solution.py:63
  55.2 0.1 pad_maximum_fusion
  55.4 0.1 fusion.6.keys_ref
  55.5 0.1 slice_negate_fusion
  55.6 0.1 fusion.2.q_ref
  55.8 15.2 %all-to-all-done.1.slab_ref = bf16[64,2,16,128]{3,2,1,0:T(8,128)(2,1)S(1)} async-done(((bf16[64,2,16,128]{3,2,1,0:T(8,128)(2,1)}), bf16[64,2,16,128]{3,2,1,0:T(8,128)(2,1)S(1)}, u32[]{:S(2)}, u32[]{:S(2)}) %all-to-all-start.1) | async-done | bytes 524320 | tf_op jit(solution)/shard_map/all_to_all | solution.py:63
  71.0 1.4 %attend.1 = bf16[128,384]{1,0:T(8,128)(2,1)S(1)} custom-call(s32[1]{0:T(128)S(6)} %copy.23.length_ref, bf16[3,128,128]{2,1,0:T(8,128)(2,1)S(1)} %fusion.2.q_ref, bf16[64,2,16,128]{3,2,1,0:T(8,128)(2,1)S(1)} %all-to-all-done.1.slab_ref, bf16[128,128]{1,0:T(8,128)(2,1)S(1)} %fusion.6.keys_ref, bf16[128,128]{1,0:T(8,128)(2,1)S(1)} %fusion.5.vals_ref), custom_call_target="tpu_custom_call" | custom-call | tf_op jit(solution)/shard_map/attend/pallas_call | solution.py:93
  72.4 24.6 %all-gather = bf16[1024,384]{1,0:T(8,128)(2,1)S(1)} all-gather(bf16[128,384]{1,0:T(8,128)(2,1)S(1)} %attend.1), channel_id=2, replica_groups=mesh['req'=64,'tp'=8] {'tp'}, dimensions={0}, use_global_device_ids=true | all-gather | bytes 884736 | tf_op jit(solution)/shard_map/all_gather | solution.py:162
  96.9 0.0 copy-done
  96.9 3.8 %project.1 = bf16[128,640]{1,0:T(8,128)(2,1)} custom-call(bf16[8,128,384]{2,1,0:T(8,128)(2,1)S(1)} %bitcast.45, bf16[3072,640]{1,0:T(8,128)(2,1)} %weight_ref.1, bf16[128,640]{1,0:T(8,128)(2,1)S(1)} %bitcast.46), custom_call_target="tpu_custom_call" | custom-call | tf_op jit(solution)/shard_map/project/pallas_call | solution.py:120
  (7 shorter events, 0.1 us)
Async XLA Ops:
  17.7 30.2 %all-to-all-start = ((bf16[64,17,2,128]{3,2,1,0:T(2,128)(2,1)}), bf16[64,17,2,128]{3,2,1,0:T(2,128)(2,1)S(1)}, u32[]{:S(2)}, u32[]{:S(2)}) async-start(bf16[64,17,2,128]{3,2,1,0:T(2,128)(2,1)} %tag_pieces.1), calls=%async_computation | async-start | bytes 1114112 | tf_op jit(solution)/shard_map/all_to_all | solution.py:54
  30.6 66.3 %copy-start = (bf16[1,128,640]{2,1,0:T(8,128)(2,1)S(1)}, bf16[1,128,640]{2,1,0:T(8,128)(2,1)}, u32[]{:S(2)}) copy-start(bf16[1,128,640]{2,1,0:T(8,128)(2,1)} %param.20) | copy-start | bytes 491524
  49.0 22.0 %all-to-all-start.1 = ((bf16[64,2,16,128]{3,2,1,0:T(8,128)(2,1)}), bf16[64,2,16,128]{3,2,1,0:T(8,128)(2,1)S(1)}, u32[]{:S(2)}, u32[]{:S(2)}) async-start(bf16[64,2,16,128]{3,2,1,0:T(8,128)(2,1)} %select_select_fusion), calls=%async_computation.1 | async-start | bytes 1048576 | tf_op jit(solution)/shard_map/all_to_all | solution.py:63

commit v3 on v2

--- a/solution.py
+++ b/solution.py
@@ -23,15 +23,14 @@
     return vectors * cosine + turned * sine
 
 
-def tag_kernel(group_ref, slab_ref, out_ref, tag_ref, sems):
+def tag_kernel(group_ref, slab_ref, out_ref, sem):
     piece = slab_ref.shape[1]
-    data = pltpu.make_async_copy(slab_ref, out_ref.at[:, pl.ds(0, piece)], sems.at[0])
+    data = pltpu.make_async_copy(slab_ref, out_ref.at[:, pl.ds(0, piece)], sem)
     data.start()
-    tag_ref[...] = jnp.full(tag_ref.shape, group_ref[0].astype(jnp.float32), jnp.float32).astype(tag_ref.dtype)
-    tags = pltpu.make_async_copy(tag_ref, out_ref.at[:, pl.ds(piece, 1)], sems.at[1])
-    tags.start()
+    shape = (out_ref.shape[0], 1) + out_ref.shape[2:]
+    group = group_ref[0].astype(jnp.float32)
+    out_ref[:, piece:] = jnp.full(shape, group, jnp.float32).astype(out_ref.dtype)
     data.wait()
-    tags.wait()
 
 
 def tagged(pieces, group):
@@ -40,9 +39,9 @@
         tag_kernel,
         out_shape=jax.ShapeDtypeStruct((columns, piece + 1, 2, HD), pieces.dtype),
         in_specs=[pl.BlockSpec(memory_space=pltpu.SMEM), pl.BlockSpec(memory_space=pltpu.HBM)],
-        out_specs=pl.BlockSpec(memory_space=pl.ANY),
-        scratch_shapes=[pltpu.VMEM((columns, 1, 2, HD), pieces.dtype), pltpu.SemaphoreType.DMA((2,))],
-        compiler_params=pltpu.CompilerParams(vmem_limit_bytes=1 << 20),
+        out_specs=pl.BlockSpec(memory_space=pltpu.VMEM),
+        scratch_shapes=[pltpu.SemaphoreType.DMA],
+        compiler_params=pltpu.CompilerParams(vmem_limit_bytes=2 << 20),
         name="tag_pieces",
     )(group, pltpu.with_memory_space_constraint(pieces, pltpu.HBM))
 
@@ -100,23 +99,31 @@
     )(length, queries, slab, keys, vals)
 
 
-def project_kernel(parts_ref, weight_ref, resid_ref, out_ref, held_ref, sems):
+HELD = 5
+
+
+def project_kernel(parts_ref, weight_ref, held_ref, resid_ref, out_ref, late_ref, sems):
     parts, _, width = parts_ref.shape
+    late = late_ref.shape[0]
     copies = [
-        pltpu.make_async_copy(weight_ref.at[pl.ds(p * width, width)], held_ref.at[p], sems.at[p])
-        for p in range(parts)
+        pltpu.make_async_copy(weight_ref.at[pl.ds(p * width, width)], late_ref.at[p], sems.at[p])
+        for p in range(late)
     ]
     for copy in copies:
         copy.start()
     total = resid_ref[...].astype(jnp.float32)
-    for p in range(parts):
+    for p in range(late, parts):
+        rows = held_ref[(p - late) * width : (p - late + 1) * width, :]
+        total += jnp.dot(parts_ref[p], rows, preferred_element_type=jnp.float32)
+    for p in range(late):
         copies[p].wait()
-        total += jnp.dot(parts_ref[p], held_ref[p], preferred_element_type=jnp.float32)
+        total += jnp.dot(parts_ref[p], late_ref[p], preferred_element_type=jnp.float32)
     out_ref[...] = total.astype(out_ref.dtype)
 
 
 def project(parts, weight, resid):
     count, _, width = parts.shape
+    late = count - HELD
     return pl.pallas_call(
         project_kernel,
         out_shape=jax.ShapeDtypeStruct(resid.shape, resid.dtype),
@@ -124,15 +131,16 @@
             pl.BlockSpec(memory_space=pltpu.VMEM),
             pl.BlockSpec(memory_space=pltpu.HBM),
             pl.BlockSpec(memory_space=pltpu.VMEM),
+            pl.BlockSpec(memory_space=pltpu.VMEM),
         ],
         out_specs=pl.BlockSpec(memory_space=pltpu.VMEM),
         scratch_shapes=[
-            pltpu.VMEM((count, width, weight.shape[1]), weight.dtype),
-            pltpu.SemaphoreType.DMA((count,)),
+            pltpu.VMEM((late, width, weight.shape[1]), weight.dtype),
+            pltpu.SemaphoreType.DMA((late,)),
         ],
-        compiler_params=pltpu.CompilerParams(vmem_limit_bytes=12 << 20),
+        compiler_params=pltpu.CompilerParams(vmem_limit_bytes=6 << 20),
         name="project",
-    )(parts, pltpu.with_memory_space_constraint(weight, pltpu.HBM), resid)
+    )(parts, pltpu.with_memory_space_constraint(weight, pltpu.HBM), weight[late * width :], resid)
 
 
 def body(

time: 101 us -> 87.2 us (0.86)
  Pallas kernels: 22.2 us -> 6.1 us
  waiting for transfers between devices: 20.4 us -> 16.6 us
  other arithmetic: 4.8 us -> 7.4 us
  local copies, waits for them, and re-layouts: 2.51 us -> 4.49 us
  starting transfers between devices: 19.2 us -> 21 us
    pallas_call x1, Pallas kernels: 17 us -> 1.85 us  [tagged(): pl.pallas_call(tag_kernel, out_shape=jax.ShapeDtypeStruct((columns, piece...]
    all_to_all x1, waiting for transfers between devices: 5.2 us -> 2.66 us  [fetch_prefix(): spread = lax.all_to_all(tagged(pieces, group), 'req', 0, 0, tiled=True)]
    slice x0 -> x1, local copies, waits for them, and re-layouts: none -> 1.91 us  [project(): weight[late * width:]]
    all_to_all x1, starting transfers between devices: 6.25 us -> 8.08 us  [fetch_prefix(): return lax.all_to_all(outgoing, 'req', 0, 0, tiled=True)]
    all_to_all x1, waiting for transfers between devices: 15.2 us -> 13.9 us  [fetch_prefix(): return lax.all_to_all(outgoing, 'req', 0, 0, tiled=True)]
  transfers between devices with their start and end apart: 2 -> 2, of which waited for: 2 -> 2; matrix products, arithmetic and copies ran while one was open for 6% -> 12% of each run, Pallas kernels for 0% -> 0%
where the time goes in v3:
time: 87.2 us; the launch traced here: 86.2 us
  blocking collectives  23.6 us (27%)
  starting transfers between devices  21 us (24%)
  waiting for transfers between devices  16.6 us (19%)
  other arithmetic  7.4 us (8%)
  between operations  6.99 us (8%)
  Pallas kernels  6.1 us (7%)
  local copies, waits for them, and re-layouts  4.49 us (5%)
    all_gather x1, blocking collectives, body(): parts = lax.all_gather(attended, 'tp', axis=0)  23.6 us
    all_to_all x1, waiting for transfers between devices, fetch_prefix(): return lax.all_to_all(outgoing, 'req', 0, 0, tiled=True)  13.9 us
    all_to_all x1, starting transfers between devices, fetch_prefix(): spread = lax.all_to_all(tagged(pieces, group), 'req', 0, 0, tiled=True)  12.9 us
    all_to_all x1, starting transfers between devices, fetch_prefix(): return lax.all_to_all(outgoing, 'req', 0, 0, tiled=True)  8.08 us
    pallas_call x1, Pallas kernels, project(): pl.pallas_call(project_kernel, out_shape=jax.ShapeDtypeStruct(resid.shape...  2.86 us
    all_to_all x1, waiting for transfers between devices, fetch_prefix(): spread = lax.all_to_all(tagged(pieces, group), 'req', 0, 0, tiled=True)  2.66 us
    slice x1, local copies, waits for them, and re-layouts, project(): weight[late * width:]  1.91 us
    pallas_call x1, Pallas kernels, tagged(): pl.pallas_call(tag_kernel, out_shape=jax.ShapeDtypeStruct((columns, piece...  1.85 us
  transfers between devices with their start and end apart: 2, of which 2 were waited for; matrix products, arithmetic and copies ran while one was open for 12% of the time, Pallas kernels for 0%

profile of v3, /device:TPU:1, one launch (start us, length us, event | category | flops | bytes accessed | tf_op | source)
XLA Modules:
  0.0 86.2 jit_solution(16154173054969959326)
XLA Ops:
  0.0 0.0 copy-start.1
  0.7 1.9 %tag_pieces.1 = bf16[64,17,2,128]{3,2,1,0:T(2,128)(2,1)} custom-call(s32[1]{0:T(128)S(6)} %copy.24.group_ref, bf16[64,16,2,128]{3,2,1,0:T(2,128)(2,1)} %bitcast.47), custom_call_target="tpu_custom_call" | custom-call | tf_op jit(solution)/shard_map/tag_pieces/pallas_call | solution.py:38
  2.5 12.9 %all-to-all-start = ((bf16[64,17,2,128]{3,2,1,0:T(2,128)(2,1)}), bf16[64,17,2,128]{3,2,1,0:T(2,128)(2,1)S(1)}, u32[]{:S(2)}, u32[]{:S(2)}) async-start(bf16[64,17,2,128]{3,2,1,0:T(2,128)(2,1)} %tag_pieces.1), calls=%async_computation | async-start | bytes 1114112 | tf_op jit(solution)/shard_map/all_to_all | solution.py:53
  15.5 1.4 %fusion.8 = (s32[1]{0:T(128)}, s32[1]{0:T(128)}, s32[1]{0:T(128)}) fusion(s32[3]{0:T(128)} %param.18), kind=kLoop, calls=%fused_computation.29 | loop fusion | bytes 24 | tf_op jit(solution)/shard_map/slice | solution.py:56
  21.2 0.7 convert_element_type.55
  21.9 0.7 bitcast_convert_fusion
  22.6 1.0 %copy.16 = bf16[1,128,384]{1,2,0:T(8,128)(2,1)S(1)} copy(bf16[1,128,384]{2,1,0:T(8,128)(2,1)} %param.11) | data formatting | bytes 196608 | tf_op args[0]
  23.6 0.1 copy.17
  23.7 1.9 %slice.70.held_ref = bf16[1920,640]{1,0:T(8,128)(2,1)S(1)} slice(bf16[3072,640]{1,0:T(8,128)(2,1)} %weight_ref.1), slice={[1152:3072], [0:640]} | slice | bytes 4915200 | tf_op jit(solution)/shard_map/slice | solution.py:143
  25.6 0.0 copy-start
  27.5 0.0 copy-done.1
  27.5 1.0 %fusion.7 = (f32[128,1,64]{2,0,1:T(8,128)}, f32[128,64]{1,0:T(8,128)}, f32[128,64]{1,0:T(8,128)}) fusion(f32[64]{0:T(128)S(1)} %multiply_exponential_fusion, f32[128]{0:T(128)S(1)} %convert_bitcast_fusion), kind=kLoop, calls=%fused_computation.22 | loop fusion | flops 8192 | bytes 99072 | tf_op jit(solution)/shard_map/concatenate | solution.py:21
  28.5 0.8 convert_add_fusion
  29.3 0.7 slice_negate_fusion.1
  30.1 2.7 %all-to-all-done = bf16[64,17,2,128]{3,2,1,0:T(2,128)(2,1)S(1)} async-done(((bf16[64,17,2,128]{3,2,1,0:T(2,128)(2,1)}), bf16[64,17,2,128]{3,2,1,0:T(2,128)(2,1)S(1)}, u32[]{:S(2)}, u32[]{:S(2)}) %all-to-all-start) | async-done | bytes 557088 | tf_op jit(solution)/shard_map/all_to_all | solution.py:53
  32.8 0.1 compare_bitcast_fusion.1
  32.9 1.0 %select_select_fusion = bf16[64,2,16,128]{3,2,1,0:T(8,128)(2,1)} fusion(pred[64,2,128]{2,1,0:T(4,128)(4,1)S(1)} %get-tuple-element.9, pred[64,2,128]{2,1,0:T(4,128)(4,1)S(1)} %get-tuple-element.8, bf16[2,16,128]{2,1,0:T(8,128)(2,1)S(1)} %copy.20, bf16[2,16,128]{2,1,0:T(8,128)(2,1)S(1)} %copy.19, bf16[2,16,128]{2,1,0:T(8,128)(2,1)S(1)} %copy.18), kind=kLoop, calls=%fused_computation | loop fusion | flops 524288 | bytes 581632 | tf_op jit(solution)/shard_map/jit(_where)/select_n | solution.py:61
  33.9 8.1 %all-to-all-start.1 = ((bf16[64,2,16,128]{3,2,1,0:T(8,128)(2,1)}), bf16[64,2,16,128]{3,2,1,0:T(8,128)(2,1)S(1)}, u32[]{:S(2)}, u32[]{:S(2)}) async-start(bf16[64,2,16,128]{3,2,1,0:T(8,128)(2,1)} %select_select_fusion), calls=%async_computation.1 | async-start | bytes 1048576 | tf_op jit(solution)/shard_map/all_to_all | solution.py:62
  42.0 1.0 %pad_maximum_fusion = (f32[128,128]{1,0:T(8,128)S(1)}, f32[128,128]{1,0:T(8,128)S(1)}) fusion(f32[128,64]{1,0:T(8,128)} %get-tuple-element.16, f32[128,64]{1,0:T(8,128)} %get-tuple-element.15), kind=kLoop, calls=%fused_computation.17 | loop fusion | flops 32768 | bytes 196608 | tf_op jit(solution)/shard_map/concatenate | solution.py:20
  43.0 1.1 %fusion.6.keys_ref = bf16[128,128]{1,0:T(8,128)(2,1)S(1)} fusion(f32[128,1,64]{2,0,1:T(8,128)} %get-tuple-element.14, f32[128,1,64]{2,0,1:T(8,128)} %get-tuple-element.13, f32[128,1,64]{2,0,1:T(8,128)} %get-tuple-element.12, f32[128,2,128]{2,0,1:T(8,128)S(1)} %convert_add_fusion, f32[128,64]{1,0:T(8,128)} %get-tuple-element.16), kind=kLoop, calls=%fused_computation.21 | loop fusion | flops 114688 | bytes 229376 | tf_op jit(solution)/shard_map/convert_element_type | solution.py:167
  44.2 0.1 slice_negate_fusion
  44.3 0.1 fusion.2.q_ref
  44.4 13.9 %all-to-all-done.1.slab_ref = bf16[64,2,16,128]{3,2,1,0:T(8,128)(2,1)S(1)} async-done(((bf16[64,2,16,128]{3,2,1,0:T(8,128)(2,1)}), bf16[64,2,16,128]{3,2,1,0:T(8,128)(2,1)S(1)}, u32[]{:S(2)}, u32[]{:S(2)}) %all-to-all-start.1) | async-done | bytes 524320 | tf_op jit(solution)/shard_map/all_to_all | solution.py:62
  58.3 1.4 %attend.1 = bf16[128,384]{1,0:T(8,128)(2,1)S(1)} custom-call(s32[1]{0:T(128)S(6)} %copy.23.length_ref, bf16[3,128,128]{2,1,0:T(8,128)(2,1)S(1)} %fusion.2.q_ref, bf16[64,2,16,128]{3,2,1,0:T(8,128)(2,1)S(1)} %all-to-all-done.1.slab_ref, bf16[128,128]{1,0:T(8,128)(2,1)S(1)} %fusion.6.keys_ref, bf16[128,128]{1,0:T(8,128)(2,1)S(1)} %fusion.5.vals_ref), custom_call_target="tpu_custom_call" | custom-call | tf_op jit(solution)/shard_map/attend/pallas_call | solution.py:92
  59.7 23.6 %all-gather = bf16[1024,384]{1,0:T(8,128)(2,1)S(1)} all-gather(bf16[128,384]{1,0:T(8,128)(2,1)S(1)} %attend.1), channel_id=2, replica_groups=mesh['req'=64,'tp'=8] {'tp'}, dimensions={0}, use_global_device_ids=true | all-gather | bytes 884736 | tf_op jit(solution)/shard_map/all_gather | solution.py:170
  83.3 0.0 copy-done
  83.3 2.9 %project.1 = bf16[128,640]{1,0:T(8,128)(2,1)} custom-call(bf16[8,128,384]{2,1,0:T(8,128)(2,1)S(1)} %bitcast.45, bf16[3072,640]{1,0:T(8,128)(2,1)} %weight_ref.1, bf16[1920,640]{1,0:T(8,128)(2,1)S(1)} %slice.70.held_ref, bf16[128,640]{1,0:T(8,128)(2,1)S(1)} %bitcast.46), custom_call_target="tpu_custom_call" | custom-call | tf_op jit(solution)/shard_map/project/pallas_call | solution.py:127
  (8 shorter events, 0.1 us)
Async XLA Ops:
  0.0 27.5 %copy-start.1 = (s32[1,128]{1,0:T(1,128)S(1)}, s32[1,128]{1,0:T(1,128)}, u32[]{:S(2)}) copy-start(s32[1,128]{1,0:T(1,128)} %param.19) | copy-start | bytes 1540
  2.5 30.2 %all-to-all-start = ((bf16[64,17,2,128]{3,2,1,0:T(2,128)(2,1)}), bf16[64,17,2,128]{3,2,1,0:T(2,128)(2,1)S(1)}, u32[]{:S(2)}, u32[]{:S(2)}) async-start(bf16[64,17,2,128]{3,2,1,0:T(2,128)(2,1)} %tag_pieces.1), calls=%async_computation | async-start | bytes 1114112 | tf_op jit(solution)/shard_map/all_to_all | solution.py:53
  25.6 57.7 %copy-start = (bf16[1,128,640]{2,1,0:T(8,128)(2,1)S(1)}, bf16[1,128,640]{2,1,0:T(8,128)(2,1)}, u32[]{:S(2)}) copy-start(bf16[1,128,640]{2,1,0:T(8,128)(2,1)} %param.20) | copy-start | bytes 491524
  33.9 24.5 %all-to-all-start.1 = ((bf16[64,2,16,128]{3,2,1,0:T(8,128)(2,1)}), bf16[64,2,16,128]{3,2,1,0:T(8,128)(2,1)S(1)}, u32[]{:S(2)}, u32[]{:S(2)}) async-start(bf16[64,2,16,128]{3,2,1,0:T(8,128)(2,1)} %select_select_fusion), calls=%async_computation.1 | async-start | bytes 1048576 | tf_op jit(solution)/shard_map/all_to_all | solution.py:62

commit v4 on v3

--- a/solution.py
+++ b/solution.py
@@ -12,15 +12,41 @@
 SCALE = 1.0 / math.sqrt(HD)
 
 
-def rotate(vectors, places):
+def turns(places):
     half = HD // 2
     index = jnp.arange(half).astype(jnp.float32)
     freqs = jnp.exp(index * (-2.0 / HD) * math.log(1000000.0))
     angles = places.astype(jnp.float32)[:, None] * freqs[None, :]
-    cosine = jnp.concatenate([jnp.cos(angles), jnp.cos(angles)], axis=-1)[:, None, :]
-    sine = jnp.concatenate([jnp.sin(angles), jnp.sin(angles)], axis=-1)[:, None, :]
-    turned = jnp.concatenate([-vectors[..., half:], vectors[..., :half]], axis=-1)
-    return vectors * cosine + turned * sine
+    cosine, sine = jnp.cos(angles), jnp.sin(angles)
+    return jnp.concatenate([cosine, cosine], axis=-1), jnp.concatenate([-sine, sine], axis=-1)
+
+
+def prepare_kernel(q_ref, kv_ref, q_bias_ref, kv_bias_ref, cos_ref, sin_ref, q_out, k_out, v_out):
+    cosine, sine = cos_ref[...], sin_ref[...]
+
+    def rotated(x):
+        return (x * cosine + pltpu.roll(x, HD // 2, 1) * sine).astype(jnp.bfloat16)
+
+    for h in range(q_out.shape[0]):
+        x = q_ref[:, h * HD : (h + 1) * HD].astype(jnp.float32)
+        q_out[h] = rotated(x + q_bias_ref[h : h + 1].astype(jnp.float32))
+    bias = kv_bias_ref[...].astype(jnp.float32)
+    k_out[...] = rotated(kv_ref[0].astype(jnp.float32) + bias[0:1])
+    v_out[...] = (kv_ref[1].astype(jnp.float32) + bias[1:2]).astype(jnp.bfloat16)
+
+
+def prepare(q_rows, kv_rows, q_bias, kv_bias, places):
+    count = q_rows.shape[0]
+    heads = q_rows.shape[1] // HD
+    flat = jax.ShapeDtypeStruct((count, HD), jnp.bfloat16)
+    return pl.pallas_call(
+        prepare_kernel,
+        out_shape=(jax.ShapeDtypeStruct((heads, count, HD), jnp.bfloat16), flat, flat),
+        in_specs=[pl.BlockSpec(memory_space=pltpu.VMEM)] * 6,
+        out_specs=(pl.BlockSpec(memory_space=pltpu.VMEM),) * 3,
+        compiler_params=pltpu.CompilerParams(vmem_limit_bytes=4 << 20),
+        name="prepare",
+    )(q_rows, jnp.swapaxes(kv_rows, 0, 1), q_bias.reshape(heads, HD), kv_bias, *turns(places))
 
 
 def tag_kernel(group_ref, slab_ref, out_ref, sem):
@@ -46,29 +72,58 @@
     )(group, pltpu.with_memory_space_constraint(pieces, pltpu.HBM))
 
 
+def choose_kernel(owner_ref, spread_ref, out_ref, held_ref, sems):
+    columns, tagged_piece = spread_ref.shape[:2]
+    piece = tagged_piece - 1
+    owned = []
+    for g in range(owner_ref.shape[0]):
+        pairs = spread_ref[owner_ref[g], pl.ds(0, piece)].astype(jnp.float32)
+        owned.append(jnp.concatenate([pairs[:, 0], pairs[:, 1]], axis=0).astype(out_ref.dtype))
+    step = columns // sems.shape[0]
+    copies = []
+    for c in range(columns):
+        tag = jnp.broadcast_to(spread_ref[c, piece, 0:1, :], owned[0].shape)
+        chosen = owned[0]
+        for g in range(1, len(owned)):
+            chosen = jnp.where(tag == float(g), owned[g], chosen)
+        held_ref[c] = chosen
+        if c % step == step - 1:
+            rows = pl.ds(c + 1 - step, step)
+            copies.append(pltpu.make_async_copy(held_ref.at[rows], out_ref.at[rows], sems.at[c // step]))
+            copies[-1].start()
+    for copy in copies:
+        copy.wait()
+
+
+def choose(owner, spread):
+    columns, tagged_piece = spread.shape[:2]
+    shape = (columns, 2 * (tagged_piece - 1), HD)
+    return pl.pallas_call(
+        choose_kernel,
+        out_shape=jax.ShapeDtypeStruct(shape, spread.dtype),
+        in_specs=[pl.BlockSpec(memory_space=pltpu.SMEM), pl.BlockSpec(memory_space=pltpu.VMEM)],
+        out_specs=pl.BlockSpec(memory_space=pltpu.HBM),
+        scratch_shapes=[pltpu.VMEM(shape, spread.dtype), pltpu.SemaphoreType.DMA((4,))],
+        compiler_params=pltpu.CompilerParams(vmem_limit_bytes=4 << 20),
+        name="choose_pieces",
+    )(owner, spread)
+
+
 def fetch_prefix(slab, group, owner):
     columns = lax.axis_size("req")
-    piece = slab.shape[0] // columns
-    pieces = slab.reshape(columns, piece, 2, HD)
+    pieces = slab.reshape(columns, slab.shape[0] // columns, 2, HD)
     spread = lax.all_to_all(tagged(pieces, group), "req", 0, 0, tiled=True)
-    groups = spread[:, piece, :, :][:, :, None, :]
-    owned = [
-        jnp.swapaxes(lax.dynamic_index_in_dim(spread, owner[g], 0, keepdims=False)[:piece], 0, 1)
-        for g in range(owner.shape[0])
-    ]
-    outgoing = jnp.broadcast_to(owned[0], (columns, 2, piece, HD))
-    for g in range(1, owner.shape[0]):
-        outgoing = jnp.where(groups == g, owned[g][None], outgoing)
-    return lax.all_to_all(outgoing, "req", 0, 0, tiled=True)
+    return lax.all_to_all(choose(owner, spread), "req", 0, 0, tiled=True)
 
 
 def attend_kernel(length_ref, q_ref, slab_ref, keys_ref, vals_ref, out_ref):
     heads, count, _ = q_ref.shape
-    prefix_len = slab_ref.shape[0] * slab_ref.shape[2]
+    piece = slab_ref.shape[1] // 2
+    prefix_len = slab_ref.shape[0] * piece
     over_d = (((1,), (1,)), ((), ()))
     over_k = (((1,), (0,)), ((), ()))
-    prefix_keys = slab_ref[:, 0].reshape(prefix_len, HD)
-    prefix_vals = slab_ref[:, 1].reshape(prefix_len, HD)
+    prefix_keys = slab_ref[:, :piece].reshape(prefix_len, HD)
+    prefix_vals = slab_ref[:, piece:].reshape(prefix_len, HD)
     row = lax.broadcasted_iota(jnp.int32, (count, count), 0)
     causal = lax.broadcasted_iota(jnp.int32, (count, count), 1) <= row
     live = lax.broadcasted_iota(jnp.int32, (count, HD), 0) < length_ref[0]
@@ -156,16 +211,8 @@
     residual,
     out_weight,
 ):
-    cap = q_proj.shape[1]
-    places = positions[0]
     slab = fetch_prefix(prefix_kv[0], group_of, owner)
-    queries = q_proj[0].astype(jnp.float32).reshape(cap, -1, HD) + q_bias.astype(
-        jnp.float32
-    ).reshape(-1, HD)
-    queries = jnp.swapaxes(rotate(queries, places).astype(jnp.bfloat16), 0, 1)
-    pairs = kv_proj[0].astype(jnp.float32) + kv_bias.astype(jnp.float32)
-    keys = rotate(pairs[:, 0][:, None, :], places)[:, 0].astype(jnp.bfloat16)
-    vals = pairs[:, 1].astype(jnp.bfloat16)
+    queries, keys, vals = prepare(q_proj[0], kv_proj[0], q_bias, kv_bias, positions[0])
     attended = attend(lengths, queries, slab, keys, vals)
     parts = lax.all_gather(attended, "tp", axis=0)
     return project(parts, out_weight, residual[0])[None]

time: 87.2 us -> 85 us (0.975)
  blocking collectives: 23.6 us -> 54.5 us
  starting transfers between devices: 21 us -> 6.26 us
  other arithmetic: 7.4 us -> 0.42 us
  between operations: 6.99 us -> 1.5 us
  waiting for transfers between devices: 16.6 us -> 12.4 us
  local copies, waits for them, and re-layouts: 4.49 us -> 2.6 us
    all_to_all x0 -> x1, blocking collectives: none -> 30 us  [fetch_prefix(): spread = lax.all_to_all(tagged(pieces, group), 'req', 0, 0, tiled=True)]
    all_to_all x2 -> x1, starting transfers between devices: 21 us -> 6.26 us  [fetch_prefix(): return lax.all_to_all(choose(owner, spread), 'req', 0, 0, tiled=True)]
    all_to_all x2 -> x1, waiting for transfers between devices: 16.6 us -> 12.4 us  [fetch_prefix(): return lax.all_to_all(choose(owner, spread), 'req', 0, 0, tiled=True)]
    concatenate x2 -> x1, other arithmetic: 2.03 us -> 0.1 us  [turns(): jnp.concatenate([cosine, cosine], axis=-1)]
    convert_element_type x3 -> x1, other arithmetic: 1.79 us -> 0.01 us  [turns(): angles = places.astype(jnp.float32)[:, None] * freqs[None, :]]
    pallas_call x0 -> x2, Pallas kernels: none -> 1.59 us  [the longest x1 1.45 us: choose(): pl.pallas_call(choose_kernel, out_shape=jax.ShapeDtypeStruct(shape, sprea...]
    add x3 -> x0, other arithmetic: 1.55 us -> none  [the longest x1 0.85 us: body(): pairs = kv_proj[0].astype(jnp.float32) + kv_bias.astype(jnp.float32)]
    slice x1 -> x0, local copies, waits for them, and re-layouts: 1.42 us -> none  [fetch_prefix(): owner[g]]
  transfers between devices with their start and end apart: 2 -> 1, of which waited for: 2 -> 1; matrix products, arithmetic and copies ran while one was open for 12% -> 3% of each run, Pallas kernels for 0% -> 0%
where the time goes in v4:
time: 85 us; the launch traced here: 84.7 us
  blocking collectives  54.5 us (64%)
  waiting for transfers between devices  12.4 us (15%)
  Pallas kernels  6.89 us (8%)
  starting transfers between devices  6.26 us (7%)
  local copies, waits for them, and re-layouts  2.6 us (3%)
  between operations  1.5 us (2%)
    all_to_all x1, blocking collectives, fetch_prefix(): spread = lax.all_to_all(tagged(pieces, group), 'req', 0, 0, tiled=True)  30 us
    all_gather x1, blocking collectives, body(): parts = lax.all_gather(attended, 'tp', axis=0)  24.6 us
    all_to_all x1, waiting for transfers between devices, fetch_prefix(): return lax.all_to_all(choose(owner, spread), 'req', 0, 0, tiled=True)  12.4 us
    all_to_all x1, starting transfers between devices, fetch_prefix(): return lax.all_to_all(choose(owner, spread), 'req', 0, 0, tiled=True)  6.26 us
    pallas_call x1, Pallas kernels, project(): pl.pallas_call(project_kernel, out_shape=jax.ShapeDtypeStruct(resid.shape...  2.86 us
    slice x1, local copies, waits for them, and re-layouts, project(): weight[late * width:]  1.91 us
  transfers between devices with their start and end apart: 1, of which 1 were waited for; matrix products, arithmetic and copies ran while one was open for 3% of the time, Pallas kernels for 0%

profile of v4, /device:TPU:1, one launch (start us, length us, event | category | flops | bytes accessed | tf_op | source)
XLA Modules:
  0.0 84.7 jit_solution(992544390870658693)
XLA Ops:
  0.0 0.0 copy-start.5
  0.7 1.1 %tag_pieces.1 = bf16[64,17,2,128]{3,2,1,0:T(2,128)(2,1)S(1)} custom-call(s32[1]{0:T(128)S(6)} %copy.16.group_ref, bf16[64,16,2,128]{3,2,1,0:T(2,128)(2,1)} %bitcast.18), custom_call_target="tpu_custom_call" | custom-call | tf_op jit(solution)/shard_map/tag_pieces/pallas_call | solution.py:64
  1.7 0.0 copy-start.6
  1.8 30.0 %all_to_all.10.spread_ref = bf16[64,17,2,128]{3,2,1,0:T(2,128)(2,1)S(1)} all-to-all(bf16[64,17,2,128]{3,2,1,0:T(2,128)(2,1)S(1)} %tag_pieces.1), channel_id=1, replica_groups=mesh['req'=64,'tp'=8] {'req'}, dimensions={0} | all-to-all | bytes 1114112 | tf_op jit(solution)/shard_map/all_to_all | solution.py:115
  31.7 0.0 copy-start.3
  31.7 0.7 copy-done.3
  32.4 0.0 copy-start.1
  32.4 0.0 copy-start.2
  32.4 0.0 copy-start.4
  32.4 1.4 %choose_pieces.1 = bf16[64,32,128]{2,1,0:T(8,128)(2,1)} custom-call(s32[3]{0:T(128)S(1)} %copy-done.3, bf16[64,17,2,128]{3,2,1,0:T(2,128)(2,1)S(1)} %all_to_all.10.spread_ref), custom_call_target="tpu_custom_call" | custom-call | tf_op jit(solution)/shard_map/choose_pieces/pallas_call | solution.py:101
  33.8 6.3 %all-to-all-start.1 = ((bf16[64,32,128]{2,1,0:T(8,128)(2,1)}), bf16[64,32,128]{2,1,0:T(8,128)(2,1)S(1)}, u32[]{:S(2)}, u32[]{:S(2)}) async-start(bf16[64,32,128]{2,1,0:T(8,128)(2,1)} %choose_pieces.1), calls=%async_computation.1 | async-start | bytes 1048576 | tf_op jit(solution)/shard_map/all_to_all | solution.py:116
  40.1 0.0 copy-start
  40.8 0.0 copy-done.5
  40.8 1.9 %slice.3.held_ref = bf16[1920,640]{1,0:T(8,128)(2,1)S(1)} slice(bf16[3072,640]{1,0:T(8,128)(2,1)} %weight_ref.1), slice={[1152:3072], [0:640]} | slice | bytes 4915200 | tf_op jit(solution)/shard_map/slice | solution.py:198
  42.8 0.0 copy-done.6
  42.8 0.3 fusion
  43.1 0.1 pad_maximum_fusion
  43.2 0.0 copy-done.1
  43.2 0.0 copy-done.2
  43.2 0.0 copy-done.4
  43.2 0.1 prepare.1
  43.4 12.4 %all-to-all-done.1.slab_ref = bf16[64,32,128]{2,1,0:T(8,128)(2,1)S(1)} async-done(((bf16[64,32,128]{2,1,0:T(8,128)(2,1)}), bf16[64,32,128]{2,1,0:T(8,128)(2,1)S(1)}, u32[]{:S(2)}, u32[]{:S(2)}) %all-to-all-start.1) | async-done | bytes 524320 | tf_op jit(solution)/shard_map/all_to_all | solution.py:116
  55.8 1.4 %attend.1 = bf16[128,384]{1,0:T(8,128)(2,1)S(1)} custom-call(s32[1]{0:T(128)S(6)} %copy.15.length_ref, bf16[3,128,128]{2,1,0:T(8,128)(2,1)S(1)} %get-tuple-element.8.q_ref, bf16[64,32,128]{2,1,0:T(8,128)(2,1)S(1)} %all-to-all-done.1.slab_ref, bf16[128,128]{1,0:T(8,128)(2,1)S(1)} %get-tuple-element.9.keys_ref, bf16[128,128]{1,0:T(8,128)(2,1)S(1)} %get-tuple-element.10.vals_ref), custom_call_target="tpu_custom_call" | custom-call | tf_op jit(solution)/shard_map/attend/pallas_call | solution.py:147
  57.2 24.6 %all-gather = bf16[1024,384]{1,0:T(8,128)(2,1)S(1)} all-gather(bf16[128,384]{1,0:T(8,128)(2,1)S(1)} %attend.1), channel_id=2, replica_groups=mesh['req'=64,'tp'=8] {'tp'}, dimensions={0}, use_global_device_ids=true | all-gather | bytes 884736 | tf_op jit(solution)/shard_map/all_gather | solution.py:217
  81.8 0.0 copy-done
  81.8 2.9 %project.1 = bf16[128,640]{1,0:T(8,128)(2,1)} custom-call(bf16[8,128,384]{2,1,0:T(8,128)(2,1)S(1)} %bitcast.13, bf16[3072,640]{1,0:T(8,128)(2,1)} %weight_ref.1, bf16[1920,640]{1,0:T(8,128)(2,1)S(1)} %slice.3.held_ref, bf16[128,640]{1,0:T(8,128)(2,1)S(1)} %bitcast.15), custom_call_target="tpu_custom_call" | custom-call | tf_op jit(solution)/shard_map/project/pallas_call | solution.py:182
  (3 shorter events, 0.0 us)
Async XLA Ops:
  0.0 40.8 %copy-start.5 = (bf16[1,128,2,128]{3,2,1,0:T(2,128)(2,1)S(1)}, bf16[1,128,2,128]{3,2,1,0:T(2,128)(2,1)}, u32[]{:S(2)}) copy-start(bf16[1,128,2,128]{3,2,1,0:T(2,128)(2,1)} %param.12) | copy-start | bytes 196612
  1.7 41.0 %copy-start.6 = (s32[1,128]{1,0:T(1,128)S(1)}, s32[1,128]{1,0:T(1,128)}, u32[]{:S(2)}) copy-start(s32[1,128]{1,0:T(1,128)} %param.19) | copy-start | bytes 1540
  31.7 0.7 copy-start.3
  32.4 10.8 %copy-start.1 = (bf16[1,128,384]{2,1,0:T(8,128)(2,1)S(1)}, bf16[1,128,384]{2,1,0:T(8,128)(2,1)}, u32[]{:S(2)}) copy-start(bf16[1,128,384]{2,1,0:T(8,128)(2,1)} %param.11) | copy-start | bytes 294916
  32.4 10.8 %copy-start.2 = (bf16[384]{0:T(512)(128)(2,1)S(1)}, bf16[384]{0:T(512)(128)(2,1)}, u32[]{:S(2)}) copy-start(bf16[384]{0:T(512)(128)(2,1)} %param.13) | copy-start | bytes 2308
  32.4 10.8 %copy-start.4 = (bf16[2,128]{1,0:T(2,128)(2,1)S(1)}, bf16[2,128]{1,0:T(2,128)(2,1)}, u32[]{:S(2)}) copy-start(bf16[2,128]{1,0:T(2,128)(2,1)} %kv_bias_ref.1) | copy-start | bytes 1540
  33.8 22.0 %all-to-all-start.1 = ((bf16[64,32,128]{2,1,0:T(8,128)(2,1)}), bf16[64,32,128]{2,1,0:T(8,128)(2,1)S(1)}, u32[]{:S(2)}, u32[]{:S(2)}) async-start(bf16[64,32,128]{2,1,0:T(8,128)(2,1)} %choose_pieces.1), calls=%async_computation.1 | async-start | bytes 1048576 | tf_op jit(solution)/shard_map/all_to_all | solution.py:116
  40.1 41.7 %copy-start = (bf16[1,128,640]{2,1,0:T(8,128)(2,1)S(1)}, bf16[1,128,640]{2,1,0:T(8,128)(2,1)}, u32[]{:S(2)}) copy-start(bf16[1,128,640]{2,1,0:T(8,128)(2,1)} %param.20) | copy-start | bytes 491524

commit v5 on v4

--- a/solution.py
+++ b/solution.py
@@ -6,9 +6,11 @@
 from jax import lax
 from jax.experimental import pallas as pl
 from jax.experimental.pallas import tpu as pltpu
-from jax.sharding import PartitionSpec as P
+from jax.sharding import Mesh, PartitionSpec as P
 
 HD = 128
+ORDER = ("y", "zl", "x")
+REQ = ("zl", "x", "y")
 SCALE = 1.0 / math.sqrt(HD)
 
 
@@ -109,11 +111,18 @@
     )(owner, spread)
 
 
+def reorder(owner):
+    y, x, zl = owner % 8, owner // 8 % 4, owner // 32
+    return (y * 2 + zl) * 4 + x
+
+
 def fetch_prefix(slab, group, owner):
-    columns = lax.axis_size("req")
+    columns = lax.axis_size(ORDER)
     pieces = slab.reshape(columns, slab.shape[0] // columns, 2, HD)
-    spread = lax.all_to_all(tagged(pieces, group), "req", 0, 0, tiled=True)
-    return lax.all_to_all(choose(owner, spread), "req", 0, 0, tiled=True)
+    owner = reorder(owner)
+    outgoing, owner = lax.optimization_barrier((tagged(pieces, group), owner))
+    spread = lax.all_to_all(outgoing, ORDER, 0, 0, tiled=True)
+    return lax.all_to_all(choose(owner, spread), ORDER, 0, 0, tiled=True)
 
 
 def attend_kernel(length_ref, q_ref, slab_ref, keys_ref, vals_ref, out_ref):
@@ -219,18 +228,19 @@
 
 
 def solution(mesh):
+    mesh = Mesh(mesh.devices.reshape(2, 4, 8, 8), REQ + ("tp",))
     in_specs = (
-        P("req", None, "tp"),
-        P("req", None, None, "tp"),
+        P(REQ, None, "tp"),
+        P(REQ, None, None, "tp"),
         P("tp"),
         P(None, "tp"),
-        P("req", None, None, "tp"),
-        P("req"),
-        P("req"),
+        P(REQ, None, None, "tp"),
+        P(REQ),
+        P(REQ),
         P(),
-        P("req", None),
-        P("req", None, "tp"),
+        P(REQ, None),
+        P(REQ, None, "tp"),
         P(None, "tp"),
     )
-    out_specs = P("req", None, "tp")
+    out_specs = P(REQ, None, "tp")
     return jax.shard_map(body, mesh=mesh, in_specs=in_specs, out_specs=out_specs, check_vma=False)

time: 85 us -> 84.4 us (level)
  starting transfers between devices: 6.26 us -> 7.35 us
    all_to_all x1, blocking collectives: 30 us -> 28.8 us  [fetch_prefix(): spread = lax.all_to_all(outgoing, ORDER, 0, 0, tiled=True)]
    all_to_all x1, starting transfers between devices: 6.26 us -> 7.35 us  [fetch_prefix(): return lax.all_to_all(choose(owner, spread), ORDER, 0, 0, tiled=True)]
    all_to_all x1, waiting for transfers between devices: 12.4 us -> 11.6 us  [fetch_prefix(): return lax.all_to_all(choose(owner, spread), ORDER, 0, 0, tiled=True)]
where the time goes in v5:
time: 84.4 us; the launch traced here: 84 us
  blocking collectives  53.7 us (64%)
  waiting for transfers between devices  11.6 us (14%)
  starting transfers between devices  7.35 us (9%)
  Pallas kernels  6.9 us (8%)
  local copies, waits for them, and re-layouts  1.95 us (2%)
  between operations  1.5 us (2%)
  other arithmetic  1.09 us (1%)
    all_to_all x1, blocking collectives, fetch_prefix(): spread = lax.all_to_all(outgoing, ORDER, 0, 0, tiled=True)  28.8 us
    all_gather x1, blocking collectives, body(): parts = lax.all_gather(attended, 'tp', axis=0)  24.8 us
    all_to_all x1, waiting for transfers between devices, fetch_prefix(): return lax.all_to_all(choose(owner, spread), ORDER, 0, 0, tiled=True)  11.6 us
    all_to_all x1, starting transfers between devices, fetch_prefix(): return lax.all_to_all(choose(owner, spread), ORDER, 0, 0, tiled=True)  7.35 us
    pallas_call x1, Pallas kernels, project(): pl.pallas_call(project_kernel, out_shape=jax.ShapeDtypeStruct(resid.shape...  2.86 us
    slice x1, local copies, waits for them, and re-layouts, project(): weight[late * width:]  1.91 us
  transfers between devices with their start and end apart: 1, of which 1 were waited for; matrix products, arithmetic and copies ran while one was open for 3% of the time, Pallas kernels for 0%

profile of v5, /device:TPU:1, one launch (start us, length us, event | category | flops | bytes accessed | tf_op | source)
XLA Modules:
  0.0 84.0 jit_solution(17883483968419309509)
XLA Ops:
  0.0 0.0 copy-start.4
  0.7 0.7 fusion.1.owner_ref
  1.4 1.1 %tag_pieces.1 = bf16[64,17,2,128]{3,2,1,0:T(2,128)(2,1)S(1)} custom-call(s32[1]{0:T(128)S(6)} %copy.16.group_ref, bf16[64,16,2,128]{3,2,1,0:T(2,128)(2,1)} %bitcast.18), custom_call_target="tpu_custom_call" | custom-call | tf_op jit(solution)/shard_map/tag_pieces/pallas_call | solution.py:66
  2.4 0.0 copy-start.5
  2.4 28.8 %all_to_all.10.spread_ref = bf16[64,17,2,128]{3,2,1,0:T(2,128)(2,1)S(1)} all-to-all(bf16[64,17,2,128]{3,2,1,0:T(2,128)(2,1)S(1)} %tag_pieces.1), channel_id=1, replica_groups=mesh['zl'=2,'x'=4,'y'=8,'tp'=8] {'y','zl','x'}, dimensions={0} | all-to-all | bytes 1114112 | tf_op jit(solution)/shard_map/all_to_all | solution.py:124
  31.3 0.0 copy-start.1
  31.3 0.0 copy-start.2
  31.3 0.0 copy-start.3
  31.3 1.5 %choose_pieces.1 = bf16[64,32,128]{2,1,0:T(8,128)(2,1)} custom-call(s32[3]{0:T(128)S(1)} %fusion.1.owner_ref, bf16[64,17,2,128]{3,2,1,0:T(2,128)(2,1)S(1)} %all_to_all.10.spread_ref), custom_call_target="tpu_custom_call" | custom-call | tf_op jit(solution)/shard_map/choose_pieces/pallas_call | solution.py:103
  32.7 7.4 %all-to-all-start.1 = ((bf16[64,32,128]{2,1,0:T(8,128)(2,1)}), bf16[64,32,128]{2,1,0:T(8,128)(2,1)S(1)}, u32[]{:S(2)}, u32[]{:S(2)}) async-start(bf16[64,32,128]{2,1,0:T(8,128)(2,1)} %choose_pieces.1), calls=%async_computation.1 | async-start | bytes 1048576 | tf_op jit(solution)/shard_map/all_to_all | solution.py:125
  40.1 0.0 copy-start
  40.8 0.0 copy-done.4
  40.8 1.9 %slice.3.held_ref = bf16[1920,640]{1,0:T(8,128)(2,1)S(1)} slice(bf16[3072,640]{1,0:T(8,128)(2,1)} %weight_ref.1), slice={[1152:3072], [0:640]} | slice | bytes 4915200 | tf_op jit(solution)/shard_map/slice | solution.py:207
  42.8 0.0 copy-done.5
  42.8 0.3 fusion
  43.1 0.1 pad_maximum_fusion
  43.2 0.0 copy-done.1
  43.2 0.0 copy-done.2
  43.2 0.0 copy-done.3
  43.2 0.1 prepare.1
  43.4 11.6 %all-to-all-done.1.slab_ref = bf16[64,32,128]{2,1,0:T(8,128)(2,1)S(1)} async-done(((bf16[64,32,128]{2,1,0:T(8,128)(2,1)}), bf16[64,32,128]{2,1,0:T(8,128)(2,1)S(1)}, u32[]{:S(2)}, u32[]{:S(2)}) %all-to-all-start.1) | async-done | bytes 524320 | tf_op jit(solution)/shard_map/all_to_all | solution.py:125
  54.9 1.4 %attend.1 = bf16[128,384]{1,0:T(8,128)(2,1)S(1)} custom-call(s32[1]{0:T(128)S(6)} %copy.15.length_ref, bf16[3,128,128]{2,1,0:T(8,128)(2,1)S(1)} %get-tuple-element.10.q_ref, bf16[64,32,128]{2,1,0:T(8,128)(2,1)S(1)} %all-to-all-done.1.slab_ref, bf16[128,128]{1,0:T(8,128)(2,1)S(1)} %get-tuple-element.13.keys_ref, bf16[128,128]{1,0:T(8,128)(2,1)S(1)} %get-tuple-element.14.vals_ref), custom_call_target="tpu_custom_call" | custom-call | tf_op jit(solution)/shard_map/attend/pallas_call | solution.py:156
  56.3 24.8 %all-gather = bf16[1024,384]{1,0:T(8,128)(2,1)S(1)} all-gather(bf16[128,384]{1,0:T(8,128)(2,1)S(1)} %attend.1), channel_id=2, replica_groups=mesh['zl'=2,'x'=4,'y'=8,'tp'=8] {'tp'}, dimensions={0}, use_global_device_ids=true | all-gather | bytes 884736 | tf_op jit(solution)/shard_map/all_gather | solution.py:226
  81.2 0.0 copy-done
  81.2 2.9 %project.1 = bf16[128,640]{1,0:T(8,128)(2,1)} custom-call(bf16[8,128,384]{2,1,0:T(8,128)(2,1)S(1)} %bitcast.13, bf16[3072,640]{1,0:T(8,128)(2,1)} %weight_ref.1, bf16[1920,640]{1,0:T(8,128)(2,1)S(1)} %slice.3.held_ref, bf16[128,640]{1,0:T(8,128)(2,1)S(1)} %bitcast.15), custom_call_target="tpu_custom_call" | custom-call | tf_op jit(solution)/shard_map/project/pallas_call | solution.py:191
  (3 shorter events, 0.0 us)
Async XLA Ops:
  0.0 40.8 %copy-start.4 = (bf16[1,128,2,128]{3,2,1,0:T(2,128)(2,1)S(1)}, bf16[1,128,2,128]{3,2,1,0:T(2,128)(2,1)}, u32[]{:S(2)}) copy-start(bf16[1,128,2,128]{3,2,1,0:T(2,128)(2,1)} %param.12) | copy-start | bytes 196612
  2.4 40.3 %copy-start.5 = (s32[1,128]{1,0:T(1,128)S(1)}, s32[1,128]{1,0:T(1,128)}, u32[]{:S(2)}) copy-start(s32[1,128]{1,0:T(1,128)} %param.19) | copy-start | bytes 1540
  31.3 11.9 %copy-start.1 = (bf16[1,128,384]{2,1,0:T(8,128)(2,1)S(1)}, bf16[1,128,384]{2,1,0:T(8,128)(2,1)}, u32[]{:S(2)}) copy-start(bf16[1,128,384]{2,1,0:T(8,128)(2,1)} %param.11) | copy-start | bytes 294916
  31.3 11.9 %copy-start.2 = (bf16[384]{0:T(512)(128)(2,1)S(1)}, bf16[384]{0:T(512)(128)(2,1)}, u32[]{:S(2)}) copy-start(bf16[384]{0:T(512)(128)(2,1)} %param.13) | copy-start | bytes 2308
  31.3 11.9 %copy-start.3 = (bf16[2,128]{1,0:T(2,128)(2,1)S(1)}, bf16[2,128]{1,0:T(2,128)(2,1)}, u32[]{:S(2)}) copy-start(bf16[2,128]{1,0:T(2,128)(2,1)} %kv_bias_ref.1) | copy-start | bytes 1540
  32.7 22.2 %all-to-all-start.1 = ((bf16[64,32,128]{2,1,0:T(8,128)(2,1)}), bf16[64,32,128]{2,1,0:T(8,128)(2,1)S(1)}, u32[]{:S(2)}, u32[]{:S(2)}) async-start(bf16[64,32,128]{2,1,0:T(8,128)(2,1)} %choose_pieces.1), calls=%async_computation.1 | async-start | bytes 1048576 | tf_op jit(solution)/shard_map/all_to_all | solution.py:125
  40.1 41.1 %copy-start = (bf16[1,128,640]{2,1,0:T(8,128)(2,1)S(1)}, bf16[1,128,640]{2,1,0:T(8,128)(2,1)}, u32[]{:S(2)}) copy-start(bf16[1,128,640]{2,1,0:T(8,128)(2,1)} %param.20) | copy-start | bytes 491524

commit v6 on v5

--- a/solution.py
+++ b/solution.py
@@ -135,20 +135,22 @@
     prefix_vals = slab_ref[:, piece:].reshape(prefix_len, HD)
     row = lax.broadcasted_iota(jnp.int32, (count, count), 0)
     causal = lax.broadcasted_iota(jnp.int32, (count, count), 1) <= row
+    causal = jnp.concatenate([causal] * heads, axis=0)
     live = lax.broadcasted_iota(jnp.int32, (count, HD), 0) < length_ref[0]
+    q = q_ref[...].reshape(heads * count, HD)
+    far = lax.dot_general(q, prefix_keys, over_d, preferred_element_type=jnp.float32)
+    near = lax.dot_general(q, keys_ref[...], over_d, preferred_element_type=jnp.float32)
+    near = jnp.where(causal, near, -1e30)
+    top = jnp.maximum(jnp.max(far, axis=-1, keepdims=True), jnp.max(near, axis=-1, keepdims=True))
+    far = jnp.exp((far - top) * SCALE)
+    near = jnp.where(causal, jnp.exp((near - top) * SCALE), 0.0)
+    total = jnp.sum(far, axis=-1, keepdims=True) + jnp.sum(near, axis=-1, keepdims=True)
+    mixed = lax.dot_general(far.astype(jnp.bfloat16), prefix_vals, over_k, preferred_element_type=jnp.float32)
+    mixed += lax.dot_general(near.astype(jnp.bfloat16), vals_ref[...], over_k, preferred_element_type=jnp.float32)
+    mixed = mixed / total
     for h in range(heads):
-        q = q_ref[h]
-        far = lax.dot_general(q, prefix_keys, over_d, preferred_element_type=jnp.float32) * SCALE
-        near = lax.dot_general(q, keys_ref[...], over_d, preferred_element_type=jnp.float32) * SCALE
-        near = jnp.where(causal, near, -1e30)
-        top = jnp.maximum(jnp.max(far, axis=-1, keepdims=True), jnp.max(near, axis=-1, keepdims=True))
-        far = jnp.exp(far - top)
-        near = jnp.where(causal, jnp.exp(near - top), 0.0)
-        total = jnp.sum(far, axis=-1, keepdims=True) + jnp.sum(near, axis=-1, keepdims=True)
-        mixed = lax.dot_general(far.astype(jnp.bfloat16), prefix_vals, over_k, preferred_element_type=jnp.float32)
-        mixed += lax.dot_general(near.astype(jnp.bfloat16), vals_ref[...], over_k, preferred_element_type=jnp.float32)
-        mixed = jnp.where(live, mixed / total, 0.0)
-        out_ref[:, h * HD : (h + 1) * HD] = mixed.astype(out_ref.dtype)
+        rows = mixed[h * count : (h + 1) * count]
+        out_ref[:, h * HD : (h + 1) * HD] = jnp.where(live, rows, 0.0).astype(out_ref.dtype)
 
 
 def attend(length, queries, slab, keys, vals):

time: 84.4 us -> 84.3 us (level)
  no operation moved by 1% of the time
where the time goes in v6:
time: 84.3 us; the launch traced here: 84 us
  blocking collectives  53.7 us (64%)
  waiting for transfers between devices  11.6 us (14%)
  starting transfers between devices  7.35 us (9%)
  Pallas kernels  6.77 us (8%)
  local copies, waits for them, and re-layouts  1.95 us (2%)
  between operations  1.5 us (2%)
  other arithmetic  1.09 us (1%)
    all_to_all x1, blocking collectives, fetch_prefix(): spread = lax.all_to_all(outgoing, ORDER, 0, 0, tiled=True)  28.8 us
    all_gather x1, blocking collectives, body(): parts = lax.all_gather(attended, 'tp', axis=0)  24.9 us
    all_to_all x1, waiting for transfers between devices, fetch_prefix(): return lax.all_to_all(choose(owner, spread), ORDER, 0, 0, tiled=True)  11.6 us
    all_to_all x1, starting transfers between devices, fetch_prefix(): return lax.all_to_all(choose(owner, spread), ORDER, 0, 0, tiled=True)  7.35 us
    pallas_call x1, Pallas kernels, project(): pl.pallas_call(project_kernel, out_shape=jax.ShapeDtypeStruct(resid.shape...  2.86 us
    slice x1, local copies, waits for them, and re-layouts, project(): weight[late * width:]  1.91 us
  transfers between devices with their start and end apart: 1, of which 1 were waited for; matrix products, arithmetic and copies ran while one was open for 3% of the time, Pallas kernels for 0%

profile of v6, /device:TPU:1, one launch (start us, length us, event | category | flops | bytes accessed | tf_op | source)
XLA Modules:
  0.0 84.0 jit_solution(2571249318146166856)
XLA Ops:
  0.0 0.0 copy-start.4
  0.7 0.7 fusion.1.owner_ref
  1.4 1.1 %tag_pieces.1 = bf16[64,17,2,128]{3,2,1,0:T(2,128)(2,1)S(1)} custom-call(s32[1]{0:T(128)S(6)} %copy.16.group_ref, bf16[64,16,2,128]{3,2,1,0:T(2,128)(2,1)} %bitcast.18), custom_call_target="tpu_custom_call" | custom-call | tf_op jit(solution)/shard_map/tag_pieces/pallas_call | solution.py:66
  2.4 0.0 copy-start.5
  2.4 28.8 %all_to_all.10.spread_ref = bf16[64,17,2,128]{3,2,1,0:T(2,128)(2,1)S(1)} all-to-all(bf16[64,17,2,128]{3,2,1,0:T(2,128)(2,1)S(1)} %tag_pieces.1), channel_id=1, replica_groups=mesh['zl'=2,'x'=4,'y'=8,'tp'=8] {'y','zl','x'}, dimensions={0} | all-to-all | bytes 1114112 | tf_op jit(solution)/shard_map/all_to_all | solution.py:124
  31.3 0.0 copy-start.1
  31.3 0.0 copy-start.2
  31.3 0.0 copy-start.3
  31.3 1.5 %choose_pieces.1 = bf16[64,32,128]{2,1,0:T(8,128)(2,1)} custom-call(s32[3]{0:T(128)S(1)} %fusion.1.owner_ref, bf16[64,17,2,128]{3,2,1,0:T(2,128)(2,1)S(1)} %all_to_all.10.spread_ref), custom_call_target="tpu_custom_call" | custom-call | tf_op jit(solution)/shard_map/choose_pieces/pallas_call | solution.py:103
  32.7 7.4 %all-to-all-start.1 = ((bf16[64,32,128]{2,1,0:T(8,128)(2,1)}), bf16[64,32,128]{2,1,0:T(8,128)(2,1)S(1)}, u32[]{:S(2)}, u32[]{:S(2)}) async-start(bf16[64,32,128]{2,1,0:T(8,128)(2,1)} %choose_pieces.1), calls=%async_computation.1 | async-start | bytes 1048576 | tf_op jit(solution)/shard_map/all_to_all | solution.py:125
  40.1 0.0 copy-start
  40.8 0.0 copy-done.4
  40.8 1.9 %slice.3.held_ref = bf16[1920,640]{1,0:T(8,128)(2,1)S(1)} slice(bf16[3072,640]{1,0:T(8,128)(2,1)} %weight_ref.1), slice={[1152:3072], [0:640]} | slice | bytes 4915200 | tf_op jit(solution)/shard_map/slice | solution.py:209
  42.8 0.0 copy-done.5
  42.8 0.3 fusion
  43.1 0.1 pad_maximum_fusion
  43.2 0.0 copy-done.1
  43.2 0.0 copy-done.2
  43.2 0.0 copy-done.3
  43.2 0.1 prepare.1
  43.4 11.6 %all-to-all-done.1.slab_ref = bf16[64,32,128]{2,1,0:T(8,128)(2,1)S(1)} async-done(((bf16[64,32,128]{2,1,0:T(8,128)(2,1)}), bf16[64,32,128]{2,1,0:T(8,128)(2,1)S(1)}, u32[]{:S(2)}, u32[]{:S(2)}) %all-to-all-start.1) | async-done | bytes 524320 | tf_op jit(solution)/shard_map/all_to_all | solution.py:125
  54.9 1.3 %attend.1 = bf16[128,384]{1,0:T(8,128)(2,1)S(1)} custom-call(s32[1]{0:T(128)S(6)} %copy.15.length_ref, bf16[3,128,128]{2,1,0:T(8,128)(2,1)S(1)} %get-tuple-element.10.q_ref, bf16[64,32,128]{2,1,0:T(8,128)(2,1)S(1)} %all-to-all-done.1.slab_ref, bf16[128,128]{1,0:T(8,128)(2,1)S(1)} %get-tuple-element.13.keys_ref, bf16[128,128]{1,0:T(8,128)(2,1)S(1)} %get-tuple-element.14.vals_ref), custom_call_target="tpu_custom_call" | custom-call | tf_op jit(solution)/shard_map/attend/pallas_call | solution.py:158
  56.2 24.9 %all-gather = bf16[1024,384]{1,0:T(8,128)(2,1)S(1)} all-gather(bf16[128,384]{1,0:T(8,128)(2,1)S(1)} %attend.1), channel_id=2, replica_groups=mesh['zl'=2,'x'=4,'y'=8,'tp'=8] {'tp'}, dimensions={0}, use_global_device_ids=true | all-gather | bytes 884736 | tf_op jit(solution)/shard_map/all_gather | solution.py:228
  81.1 0.0 copy-done
  81.1 2.9 %project.1 = bf16[128,640]{1,0:T(8,128)(2,1)} custom-call(bf16[8,128,384]{2,1,0:T(8,128)(2,1)S(1)} %bitcast.13, bf16[3072,640]{1,0:T(8,128)(2,1)} %weight_ref.1, bf16[1920,640]{1,0:T(8,128)(2,1)S(1)} %slice.3.held_ref, bf16[128,640]{1,0:T(8,128)(2,1)S(1)} %bitcast.15), custom_call_target="tpu_custom_call" | custom-call | tf_op jit(solution)/shard_map/project/pallas_call | solution.py:193
  (3 shorter events, 0.0 us)
Async XLA Ops:
  0.0 40.8 %copy-start.4 = (bf16[1,128,2,128]{3,2,1,0:T(2,128)(2,1)S(1)}, bf16[1,128,2,128]{3,2,1,0:T(2,128)(2,1)}, u32[]{:S(2)}) copy-start(bf16[1,128,2,128]{3,2,1,0:T(2,128)(2,1)} %param.12) | copy-start | bytes 196612
  2.4 40.3 %copy-start.5 = (s32[1,128]{1,0:T(1,128)S(1)}, s32[1,128]{1,0:T(1,128)}, u32[]{:S(2)}) copy-start(s32[1,128]{1,0:T(1,128)} %param.19) | copy-start | bytes 1540
  31.3 11.9 %copy-start.1 = (bf16[1,128,384]{2,1,0:T(8,128)(2,1)S(1)}, bf16[1,128,384]{2,1,0:T(8,128)(2,1)}, u32[]{:S(2)}) copy-start(bf16[1,128,384]{2,1,0:T(8,128)(2,1)} %param.11) | copy-start | bytes 294916
  31.3 11.9 %copy-start.2 = (bf16[384]{0:T(512)(128)(2,1)S(1)}, bf16[384]{0:T(512)(128)(2,1)}, u32[]{:S(2)}) copy-start(bf16[384]{0:T(512)(128)(2,1)} %param.13) | copy-start | bytes 2308
  31.3 11.9 %copy-start.3 = (bf16[2,128]{1,0:T(2,128)(2,1)S(1)}, bf16[2,128]{1,0:T(2,128)(2,1)}, u32[]{:S(2)}) copy-start(bf16[2,128]{1,0:T(2,128)(2,1)} %kv_bias_ref.1) | copy-start | bytes 1540
  32.7 22.2 %all-to-all-start.1 = ((bf16[64,32,128]{2,1,0:T(8,128)(2,1)}), bf16[64,32,128]{2,1,0:T(8,128)(2,1)S(1)}, u32[]{:S(2)}, u32[]{:S(2)}) async-start(bf16[64,32,128]{2,1,0:T(8,128)(2,1)} %choose_pieces.1), calls=%async_computation.1 | async-start | bytes 1048576 | tf_op jit(solution)/shard_map/all_to_all | solution.py:125
  40.1 41.0 %copy-start = (bf16[1,128,640]{2,1,0:T(8,128)(2,1)S(1)}, bf16[1,128,640]{2,1,0:T(8,128)(2,1)}, u32[]{:S(2)}) copy-start(bf16[1,128,640]{2,1,0:T(8,128)(2,1)} %param.20) | copy-start | bytes 491524

commit v7 on v6

--- a/solution.py
+++ b/solution.py
@@ -105,7 +105,7 @@
         out_shape=jax.ShapeDtypeStruct(shape, spread.dtype),
         in_specs=[pl.BlockSpec(memory_space=pltpu.SMEM), pl.BlockSpec(memory_space=pltpu.VMEM)],
         out_specs=pl.BlockSpec(memory_space=pltpu.HBM),
-        scratch_shapes=[pltpu.VMEM(shape, spread.dtype), pltpu.SemaphoreType.DMA((4,))],
+        scratch_shapes=[pltpu.VMEM(shape, spread.dtype), pltpu.SemaphoreType.DMA((8,))],
         compiler_params=pltpu.CompilerParams(vmem_limit_bytes=4 << 20),
         name="choose_pieces",
     )(owner, spread)

time: 84.3 us -> 84.3 us (level)
  no operation moved by 1% of the time
where the time goes in v7:
time: 84.3 us; the launch traced here: 83.9 us
  blocking collectives  53.7 us (64%)
  waiting for transfers between devices  11.6 us (14%)
  starting transfers between devices  7.35 us (9%)
  Pallas kernels  6.79 us (8%)
  local copies, waits for them, and re-layouts  1.95 us (2%)
  between operations  1.5 us (2%)
  other arithmetic  1.09 us (1%)
    all_to_all x1, blocking collectives, fetch_prefix(): spread = lax.all_to_all(outgoing, ORDER, 0, 0, tiled=True)  28.8 us
    all_gather x1, blocking collectives, body(): parts = lax.all_gather(attended, 'tp', axis=0)  24.8 us
    all_to_all x1, waiting for transfers between devices, fetch_prefix(): return lax.all_to_all(choose(owner, spread), ORDER, 0, 0, tiled=True)  11.6 us
    all_to_all x1, starting transfers between devices, fetch_prefix(): return lax.all_to_all(choose(owner, spread), ORDER, 0, 0, tiled=True)  7.35 us
    pallas_call x1, Pallas kernels, project(): pl.pallas_call(project_kernel, out_shape=jax.ShapeDtypeStruct(resid.shape...  2.86 us
    slice x1, local copies, waits for them, and re-layouts, project(): weight[late * width:]  1.91 us
  transfers between devices with their start and end apart: 1, of which 1 were waited for; matrix products, arithmetic and copies ran while one was open for 3% of the time, Pallas kernels for 0%

profile of v7, /device:TPU:1, one launch (start us, length us, event | category | flops | bytes accessed | tf_op | source)
XLA Modules:
  0.0 83.9 jit_solution(3429759577339935485)
XLA Ops:
  0.0 0.0 copy-start.4
  0.7 0.7 fusion.1.owner_ref
  1.4 1.1 %tag_pieces.1 = bf16[64,17,2,128]{3,2,1,0:T(2,128)(2,1)S(1)} custom-call(s32[1]{0:T(128)S(6)} %copy.16.group_ref, bf16[64,16,2,128]{3,2,1,0:T(2,128)(2,1)} %bitcast.18), custom_call_target="tpu_custom_call" | custom-call | tf_op jit(solution)/shard_map/tag_pieces/pallas_call | solution.py:66
  2.4 0.0 copy-start.5
  2.4 28.8 %all_to_all.10.spread_ref = bf16[64,17,2,128]{3,2,1,0:T(2,128)(2,1)S(1)} all-to-all(bf16[64,17,2,128]{3,2,1,0:T(2,128)(2,1)S(1)} %tag_pieces.1), channel_id=1, replica_groups=mesh['zl'=2,'x'=4,'y'=8,'tp'=8] {'y','zl','x'}, dimensions={0} | all-to-all | bytes 1114112 | tf_op jit(solution)/shard_map/all_to_all | solution.py:124
  31.3 0.0 copy-start.1
  31.3 0.0 copy-start.2
  31.3 0.0 copy-start.3
  31.3 1.5 %choose_pieces.1 = bf16[64,32,128]{2,1,0:T(8,128)(2,1)} custom-call(s32[3]{0:T(128)S(1)} %fusion.1.owner_ref, bf16[64,17,2,128]{3,2,1,0:T(2,128)(2,1)S(1)} %all_to_all.10.spread_ref), custom_call_target="tpu_custom_call" | custom-call | tf_op jit(solution)/shard_map/choose_pieces/pallas_call | solution.py:103
  32.8 7.4 %all-to-all-start.1 = ((bf16[64,32,128]{2,1,0:T(8,128)(2,1)}), bf16[64,32,128]{2,1,0:T(8,128)(2,1)S(1)}, u32[]{:S(2)}, u32[]{:S(2)}) async-start(bf16[64,32,128]{2,1,0:T(8,128)(2,1)} %choose_pieces.1), calls=%async_computation.1 | async-start | bytes 1048576 | tf_op jit(solution)/shard_map/all_to_all | solution.py:125
  40.1 0.0 copy-start
  40.8 0.0 copy-done.4
  40.9 1.9 %slice.3.held_ref = bf16[1920,640]{1,0:T(8,128)(2,1)S(1)} slice(bf16[3072,640]{1,0:T(8,128)(2,1)} %weight_ref.1), slice={[1152:3072], [0:640]} | slice | bytes 4915200 | tf_op jit(solution)/shard_map/slice | solution.py:209
  42.8 0.0 copy-done.5
  42.8 0.3 fusion
  43.1 0.1 pad_maximum_fusion
  43.2 0.0 copy-done.1
  43.2 0.0 copy-done.2
  43.2 0.0 copy-done.3
  43.3 0.1 prepare.1
  43.4 11.6 %all-to-all-done.1.slab_ref = bf16[64,32,128]{2,1,0:T(8,128)(2,1)S(1)} async-done(((bf16[64,32,128]{2,1,0:T(8,128)(2,1)}), bf16[64,32,128]{2,1,0:T(8,128)(2,1)S(1)}, u32[]{:S(2)}, u32[]{:S(2)}) %all-to-all-start.1) | async-done | bytes 524320 | tf_op jit(solution)/shard_map/all_to_all | solution.py:125
  55.0 1.3 %attend.1 = bf16[128,384]{1,0:T(8,128)(2,1)S(1)} custom-call(s32[1]{0:T(128)S(6)} %copy.15.length_ref, bf16[3,128,128]{2,1,0:T(8,128)(2,1)S(1)} %get-tuple-element.10.q_ref, bf16[64,32,128]{2,1,0:T(8,128)(2,1)S(1)} %all-to-all-done.1.slab_ref, bf16[128,128]{1,0:T(8,128)(2,1)S(1)} %get-tuple-element.13.keys_ref, bf16[128,128]{1,0:T(8,128)(2,1)S(1)} %get-tuple-element.14.vals_ref), custom_call_target="tpu_custom_call" | custom-call | tf_op jit(solution)/shard_map/attend/pallas_call | solution.py:158
  56.2 24.8 %all-gather = bf16[1024,384]{1,0:T(8,128)(2,1)S(1)} all-gather(bf16[128,384]{1,0:T(8,128)(2,1)S(1)} %attend.1), channel_id=2, replica_groups=mesh['zl'=2,'x'=4,'y'=8,'tp'=8] {'tp'}, dimensions={0}, use_global_device_ids=true | all-gather | bytes 884736 | tf_op jit(solution)/shard_map/all_gather | solution.py:228
  81.1 0.0 copy-done
  81.1 2.9 %project.1 = bf16[128,640]{1,0:T(8,128)(2,1)} custom-call(bf16[8,128,384]{2,1,0:T(8,128)(2,1)S(1)} %bitcast.13, bf16[3072,640]{1,0:T(8,128)(2,1)} %weight_ref.1, bf16[1920,640]{1,0:T(8,128)(2,1)S(1)} %slice.3.held_ref, bf16[128,640]{1,0:T(8,128)(2,1)S(1)} %bitcast.15), custom_call_target="tpu_custom_call" | custom-call | tf_op jit(solution)/shard_map/project/pallas_call | solution.py:193
  (3 shorter events, 0.0 us)
Async XLA Ops:
  0.0 40.8 %copy-start.4 = (bf16[1,128,2,128]{3,2,1,0:T(2,128)(2,1)S(1)}, bf16[1,128,2,128]{3,2,1,0:T(2,128)(2,1)}, u32[]{:S(2)}) copy-start(bf16[1,128,2,128]{3,2,1,0:T(2,128)(2,1)} %param.12) | copy-start | bytes 196612
  2.4 40.4 %copy-start.5 = (s32[1,128]{1,0:T(1,128)S(1)}, s32[1,128]{1,0:T(1,128)}, u32[]{:S(2)}) copy-start(s32[1,128]{1,0:T(1,128)} %param.19) | copy-start | bytes 1540
  31.3 11.9 %copy-start.1 = (bf16[1,128,384]{2,1,0:T(8,128)(2,1)S(1)}, bf16[1,128,384]{2,1,0:T(8,128)(2,1)}, u32[]{:S(2)}) copy-start(bf16[1,128,384]{2,1,0:T(8,128)(2,1)} %param.11) | copy-start | bytes 294916
  31.3 12.0 %copy-start.2 = (bf16[384]{0:T(512)(128)(2,1)S(1)}, bf16[384]{0:T(512)(128)(2,1)}, u32[]{:S(2)}) copy-start(bf16[384]{0:T(512)(128)(2,1)} %param.13) | copy-start | bytes 2308
  31.3 12.0 %copy-start.3 = (bf16[2,128]{1,0:T(2,128)(2,1)S(1)}, bf16[2,128]{1,0:T(2,128)(2,1)}, u32[]{:S(2)}) copy-start(bf16[2,128]{1,0:T(2,128)(2,1)} %kv_bias_ref.1) | copy-start | bytes 1540
  32.8 22.2 %all-to-all-start.1 = ((bf16[64,32,128]{2,1,0:T(8,128)(2,1)}), bf16[64,32,128]{2,1,0:T(8,128)(2,1)S(1)}, u32[]{:S(2)}, u32[]{:S(2)}) async-start(bf16[64,32,128]{2,1,0:T(8,128)(2,1)} %choose_pieces.1), calls=%async_computation.1 | async-start | bytes 1048576 | tf_op jit(solution)/shard_map/all_to_all | solution.py:125
  40.1 40.9 %copy-start = (bf16[1,128,640]{2,1,0:T(8,128)(2,1)S(1)}, bf16[1,128,640]{2,1,0:T(8,128)(2,1)}, u32[]{:S(2)}) copy-start(bf16[1,128,640]{2,1,0:T(8,128)(2,1)} %param.20) | copy-start | bytes 491524
